TPU v7x, 128 devices: a whole 4x4x4 slice. The times are simulated.
128 devices in a mesh: skyx: 8 (over x, core), skyy: 16 (over z, y).
Axes of the slice: x: 4, y: 4, z: 4, core: 2. Of those that a mesh axis runs over, the one named last changes fastest.
Arguments:
- tiles: bfloat16 [16384, 6, 4096], P(('skyx', 'skyy')), may hold values from -6 to 6
- tile_weight: bfloat16 [16384, 6], P(('skyx', 'skyy')), may hold values from 0.25 to 4
- owners: int32 [16384, 1], P(('skyx', 'skyy')), may hold values from 0 to 127; in each aligned block of 128 rows (0 to 127, 128 to 255, ...) at most 2 rows name the same one
- cells: int32 [16384], P(('skyx', 'skyy')), may hold values from 0 to 3
- psf_kernel: float32 [6, 9, 9], replicated, may hold values from -0.72 to 0.72
- conv1_weight: bfloat16 [64, 6, 3, 3], replicated, may hold values from -0.875 to 0.875
- conv1_bias: float32 [64], replicated, may hold values from -3 to 3
- conv2_weight: bfloat16 [64, 64, 3, 3], replicated, may hold values from -0.25 to 0.25
- conv2_bias: float32 [64], replicated, may hold values from -3 to 3
Outputs:
- psf_image: bfloat16 [6, 2048, 1024], P(None, 'skyy', 'skyx')
- detection: bfloat16 [64, 2048, 1024], P(None, 'skyy', 'skyx')
Inputs may be any that keep to these rules, and one draw needn't show every extreme that they name: `owners`: among the 128 tiles of one device at most 2 name the same owner, and every owner is named by some tile.
All inputs are finite; a program needn't handle non-finite values.
Results may differ from a plain program's by a relative error of at most 0.0035.
Values may be sent and summed in bfloat16 or wider, within the bound.
A program may use at most 192 MiB of HBM per device.

v0:
```python
import jax
import jax.numpy as jnp
from jax import lax
from jax.sharding import PartitionSpec as P

S = 64
G = 2


def extended(array, sides, width):
    for axis, dim in sides:
        size, length = (lax.axis_size(axis), array.shape[dim])
        up = [(i, (i + 1) % size) for i in range(size - 1)]
        down = [(j, i) for i, j in up]
        last = lax.slice_in_dim(array, length - width, length, axis=dim)
        first = lax.slice_in_dim(array, 0, width, axis=dim)
        before = lax.ppermute(last, axis, up)
        after = lax.ppermute(first, axis, down)
        array = jnp.concatenate([before, array, after], axis=dim)
    return array


def psf_apply(padded, kernel):
    out_height = padded.shape[1] - 8
    out_width = padded.shape[2] - 8
    summed = jnp.zeros((padded.shape[0], out_height, out_width), jnp.float32)
    for row_shift in range(9):
        for col_shift in range(9):
            summed = (
                summed
                + kernel[:, row_shift, col_shift][:, None, None]
                * padded[:, row_shift : row_shift + out_height, col_shift : col_shift + out_width]
            )
    return summed


def conv_three(padded, weight, offset):
    out_height = padded.shape[1] - 2
    out_width = padded.shape[2] - 2
    summed = jnp.zeros((weight.shape[0], out_height, out_width), jnp.float32)
    for row_shift in range(3):
        for col_shift in range(3):
            summed = summed + jnp.einsum(
                "oi,iyx->oyx",
                weight[:, :, row_shift, col_shift],
                padded[:, row_shift : row_shift + out_height, col_shift : col_shift + out_width],
                preferred_element_type=jnp.float32,
            )
    return summed + offset[:, None, None]


def accumulate(received):
    got_tiles, got_weight, got_code = received
    band_count = got_tiles.shape[-2]
    pixel_area = got_tiles.shape[-1]
    flat_tiles = got_tiles.reshape(-1, band_count, pixel_area)
    flat_weight = got_weight.reshape(-1, band_count)
    flat_code = got_code.reshape(-1, band_count)
    block_ids = jnp.arange(G * G, dtype=jnp.int32).astype(jnp.bfloat16)[:, None, None]
    coeffs = jnp.where(
        flat_code[None] == block_ids, flat_weight[None], jnp.zeros_like(flat_weight)[None]
    )
    numer = jnp.einsum("cmb,mbp->cbp", coeffs, flat_tiles, preferred_element_type=jnp.float32)
    denom = jnp.sum(coeffs.astype(jnp.float32), axis=1)
    return (numer, denom)


def body(
    tiles,
    tile_weight,
    owners,
    cells,
    psf_kernel,
    conv1_weight,
    conv1_bias,
    conv2_weight,
    conv2_bias,
):
    devices_x = lax.axis_size("skyx")
    devices_y = lax.axis_size("skyy")
    devices = devices_x * devices_y
    tile_count = tiles.shape[0]
    band_count = tiles.shape[1]
    pixel_area = tiles.shape[2]
    capacity = max(2, 2 * tile_count // devices)
    owner = owners[:, 0]
    member = (owner[:, None] == jnp.arange(devices, dtype=jnp.int32)[None, :]).astype(jnp.float32)
    earlier = (jnp.arange(tile_count)[None, :] < jnp.arange(tile_count)[:, None]).astype(
        jnp.float32
    )
    preceding = jnp.dot(earlier, member, precision=lax.Precision.HIGHEST)
    position_rank = jnp.sum(preceding * member, axis=1).astype(jnp.int32)
    slot_index = owner * capacity + position_rank
    selector = (
        slot_index[None, :] == jnp.arange(devices * capacity, dtype=jnp.int32)[:, None]
    ).astype(jnp.bfloat16)
    sent_tiles = jnp.dot(
        selector,
        tiles.reshape(tile_count, band_count * pixel_area),
        preferred_element_type=jnp.float32,
    ).astype(jnp.bfloat16)
    sent_weight = jnp.dot(selector, tile_weight, preferred_element_type=jnp.float32).astype(
        jnp.bfloat16
    )
    marker = (
        jnp.dot(
            selector, (cells + 1).astype(jnp.bfloat16)[:, None], preferred_element_type=jnp.float32
        )
        - 1.0
    )
    sent_code = jnp.broadcast_to(marker, (devices * capacity, band_count)).astype(jnp.bfloat16)
    numer, denom = accumulate(
        (
            lax.all_to_all(
                sent_tiles.reshape(devices, capacity, band_count, pixel_area),
                ("skyx", "skyy"),
                split_axis=0,
                concat_axis=0,
                tiled=True,
            ),
            lax.all_to_all(
                sent_weight.reshape(devices, capacity, band_count),
                ("skyx", "skyy"),
                split_axis=0,
                concat_axis=0,
                tiled=True,
            ),
            lax.all_to_all(
                sent_code.reshape(devices, capacity, band_count),
                ("skyx", "skyy"),
                split_axis=0,
                concat_axis=0,
                tiled=True,
            ),
        )
    )
    coadd = numer / (1.0 + denom)[:, :, None]
    patch = G * S
    coadd_image = (
        coadd.reshape(G, G, band_count, S, S)
        .transpose(2, 0, 3, 1, 4)
        .reshape(band_count, patch, patch)
    )
    padded = extended(coadd_image, (("skyx", 2), ("skyy", 1)), 4)
    psf_image = psf_apply(padded, psf_kernel).astype(jnp.bfloat16)
    padded_psf = extended(psf_image, (("skyx", 2), ("skyy", 1)), 1)
    hidden = jax.nn.silu(conv_three(padded_psf, conv1_weight, conv1_bias)).astype(jnp.bfloat16)
    padded_hidden = extended(hidden, (("skyx", 2), ("skyy", 1)), 1)
    detection = conv_three(padded_hidden, conv2_weight, conv2_bias).astype(jnp.bfloat16)
    return (psf_image, detection)


def solution(mesh):
    in_specs = (
        P(("skyx", "skyy"), None, None),
        P(("skyx", "skyy"), None),
        P(("skyx", "skyy"), None),
        P(("skyx", "skyy")),
        P(),
        P(),
        P(),
        P(),
        P(),
    )
    out_specs = (P(None, "skyy", "skyx"), P(None, "skyy", "skyx"))
    return jax.shard_map(body, mesh=mesh, in_specs=in_specs, out_specs=out_specs, check_vma=False)
```

profile of v0, /device:TPU:69, one launch (start us, length us, event | category | flops | bytes accessed | tf_op | source)
XLA Modules:
  0.0 454.8 jit_solution(12551516524323820537)
XLA Ops:
  0.6 0.9 fusion.26
  2.2 0.8 fusion.133
  3.2 0.8 broadcast_in_dim.23
  4.0 10.3 %all-to-all-start.1 = ((bf16[128,2,6]{2,1,0:T(2,128)(2,1)}), bf16[128,2,6]{2,1,0:T(2,128)(2,1)S(1)}, u32[]{:S(2)}, u32[]{:S(2)}) async-start(bf16[128,2,6]{2,1,0:T(2,128)(2,1)} %broadcast_in_dim.23), calls=%async_computation.1 | async-start | bytes 131072 | tf_op jit(solution)/shard_map/all_to_all | solution.py:128
  14.5 0.8 copy.107
  15.3 8.7 %copy.103 = bf16[128,6,4096]{0,2,1:T(8,128)(2,1)} copy(bf16[128,6,4096]{2,0,1:T(8,128)(2,1)} %param.9) | data formatting | bytes 12582912 | tf_op args[0]
  24.0 9.8 %all-to-all-start.2 = ((bf16[128,2,6]{2,1,0:T(2,128)(2,1)}), bf16[128,2,6]{2,1,0:T(2,128)(2,1)S(1)}, u32[]{:S(2)}, u32[]{:S(2)}) async-start(bf16[128,2,6]{2,1,0:T(2,128)(2,1)} %bitcast.5), calls=%async_computation.2 | async-start | bytes 131072 | tf_op jit(solution)/shard_map/all_to_all | solution.py:121
  33.7 9.2 %convolution_convert_fusion = bf16[256,24576]{1,0:T(8,128)(2,1)} fusion(bf16[128,24576]{0,1:T(8,128)(2,1)} %bitcast.131, s32[128]{0:T(128)S(1)} %convert_add_fusion), kind=kOutput, calls=%fused_computation | convolution fusion | flops 1616936960 | bytes 18874880 | tf_op jit(solution)/shard_map/dot_general | solution.py:97
  42.9 23.8 %reshape.53 = bf16[128,2,6,4096]{3,2,1,0:T(8,128)(2,1)} reshape(bf16[256,24576]{1,0:T(8,128)(2,1)} %convolution_convert_fusion) | data formatting | bytes 25165824 | tf_op jit(solution)/shard_map/reshape | solution.py:115
  66.7 19.2 %copy.104 = bf16[128,2,6,4096]{3,1,2,0:T(2,128)(2,1)} copy(bf16[128,2,6,4096]{3,2,1,0:T(8,128)(2,1)} %reshape.53) | data formatting | bytes 25165824 | tf_op jit(solution)/shard_map/reshape | solution.py:115
  86.0 10.8 %all-to-all-start = ((bf16[128,2,6,4096]{3,1,2,0:T(2,128)(2,1)}), bf16[128,2,6,4096]{3,1,2,0:T(2,128)(2,1)}, u32[]{:S(2)}, u32[]{:S(2)}) async-start(bf16[128,2,6,4096]{3,1,2,0:T(2,128)(2,1)} %copy.104), calls=%async_computation | async-start | bytes 25165824 | tf_op jit(solution)/shard_map/all_to_all | solution.py:114
  96.8 1.0 slice_reduce_fusion.78
  97.8 1.1 slice_reduce_fusion.79
  98.9 1.1 slice_reduce_fusion.80
  100.0 1.0 slice_reduce_fusion.77
  101.4 151.1 %all-to-all-done = bf16[128,2,6,4096]{3,1,2,0:T(2,128)(2,1)} async-done(((bf16[128,2,6,4096]{3,1,2,0:T(2,128)(2,1)}), bf16[128,2,6,4096]{3,1,2,0:T(2,128)(2,1)}, u32[]{:S(2)}, u32[]{:S(2)}) %all-to-all-start) | async-done | bytes 12582944 | tf_op jit(solution)/shard_map/all_to_all | solution.py:114
  252.5 12.9 %copy.105 = bf16[128,2,6,4096]{3,1,0,2:T(2,128)(2,1)} copy(bf16[128,2,6,4096]{3,1,2,0:T(2,128)(2,1)} %all-to-all-done) | data formatting | bytes 25165824 | tf_op jit(solution)/shard_map/all_to_all | solution.py:114
  265.4 19.0 %reshape.54 = bf16[256,6,4096]{2,0,1:T(8,128)(2,1)} reshape(bf16[128,2,6,4096]{3,1,0,2:T(2,128)(2,1)} %copy.105) | data formatting | bytes 25165824 | tf_op jit(solution)/shard_map/reshape | solution.py:56
  284.4 6.3 %fusion = f32[4,6,4096]{2,0,1:T(4,128)S(1)} fusion(bf16[256,6,4096]{2,0,1:T(8,128)(2,1)} %reshape.54, f32[4,6]{0,1:T(8,128)S(1)} %broadcast_add_fusion, bf16[256,6]{0,1:T(8,128)(2,1)S(1)} %copy.108, bf16[256,6]{0,1:T(8,128)(2,1)S(1)} %copy.106, bf16[4]{0:T(256)(128)(2,1)S(1)} %iota_convert_fusion), kind=kOutput, calls=%fused_computation.2 | convolution fusion | flops 50454528 | bytes 12982376 | tf_op jit(solution)/shard_map/cmb,mbp->cbp/dot_general | solution.py:63
  292.7 1.9 collective-permute-start
  294.6 4.5 collective-permute-start.1
  299.1 0.8 slice_reduce_fusion.76
  300.7 4.7 %collective-permute-done.1 = f32[6,128,4]{2,0,1:T(8,128)S(1)} collective-permute-done((f32[6,128,4]{2,0,1:T(8,128)S(1)}, f32[6,128,4]{2,0,1:T(8,128)S(1)}, u32[]{:S(2)}, u32[]{:S(2)}) %collective-permute-start.1) | collective-permute-done | bytes 12320 | tf_op jit(solution)/shard_map/ppermute | solution.py:18
  305.5 9.3 %collective-permute-start.2 = (f32[6,4,136]{2,0,1:T(8,128)S(1)}, f32[6,4,136]{2,0,1:T(8,128)S(1)}, u32[]{:S(2)}, u32[]{:S(2)}) collective-permute-start(f32[6,4,136]{2,0,1:T(8,128)S(1)} %get-tuple-element.99), channel_id=1, source_target_pairs={{0,1},{1,2},{2,3},{3,4},{4,5},{5,6},{6,7},{7,8},{8,9},{9,10},{10,1... | collective-permute-start | bytes 39176 | tf_op jit(solution)/shard_map/ppermute | solution.py:17
  314.8 2.1 collective-permute-start.3
  316.9 0.9 copy-done.4
  317.9 1.6 collective-permute-done.3
  319.4 0.9 maximum_maximum_fusion.1
  320.3 13.8 %fusion.57 = bf16[6,128,128]{2,0,1:T(8,128)(2,1)S(1)} fusion(f32[6,132,136]{2,0,1:T(8,128)S(1)} %get-tuple-element.98, f32[6,128,128]{2,0,1:T(8,128)S(1)} %get-tuple-element.108, f32[6,128,4]{2,0,1:T(8,128)S(1)} %collective-permute-done, f32[6,128,132]{2,0,1:T(8,128)} %copy-done.4, f32[6,132,136]{2,0,1:T(8,128)S(1)} %get-tuple-element.97, ...), kind=kLoop, calls=%fused_computation.76 | loop fusion | flops 16318464 | bytes 30488472 | tf_op jit(solution)/shard_map/convert_element_type | solution.py:145
  334.3 3.0 collective-permute-start.4
  337.3 1.9 collective-permute-start.5
  339.2 0.7 fusion.161
  340.7 4.3 collective-permute-done.5
  345.0 1.9 collective-permute-start.6
  347.0 5.6 %collective-permute-start.7 = (bf16[6,1,130]{2,0,1:T(8,128)(2,1)S(1)}, bf16[6,1,130]{2,0,1:T(8,128)(2,1)S(1)}, u32[]{:S(2)}, u32[]{:S(2)}) collective-permute-start(bf16[6,1,130]{2,0,1:T(8,128)(2,1)S(1)} %get-tuple-element.104), channel_id=1, source_target_pairs={{1,0},{2,1},{3,2},{4,3},{5,4},{6,5},{7,6},{8,7},{9,8},{10,9},{11,1... | collective-permute-start | bytes 4688 | tf_op jit(solution)/shard_map/ppermute | solution.py:18
  352.6 0.8 fusion.125
  353.4 0.8 fusion.123
  354.7 2.7 fusion.127
  357.4 2.7 fusion.129
  360.1 2.7 fusion.131
  362.8 2.7 fusion.119
  365.5 2.7 fusion.121
  368.2 8.7 %fusion.4 = bf16[64,128,128]{2,0,1:T(8,128)(2,1)S(1)} fusion(f32[128,128,64]{1,2,0:T(8,128)} %fusion.119, f32[128,128,64]{1,2,0:T(8,128)} %fusion.121, f32[128,128,64]{1,2,0:T(8,128)S(1)} %fusion.123, f32[128,128,64]{1,2,0:T(8,128)S(1)} %fusion.161, f32[128,128,64]{1,2,0:T(8,128)S(1)} %fusion.125, f32[128,128,64]{1,2,0:T(8,128)} %fusion.127, ...), kind=kOutput, calls=%fused_computation.11 | convolution fusion | flops 27262976 | bytes 35917312 | tf_op jit(solution)/shard_map/oi,iyx->oyx/dot_general | solution.py:43
  377.0 2.9 fusion.172
  379.9 3.7 copy.126
  383.6 1.9 collective-permute-start.9
  385.5 2.7 fusion.142
  388.1 3.7 copy.125
  391.8 3.9 collective-permute-start.8
  395.7 3.9 copy.128
  399.6 5.0 %fusion.13 = f32[128,128,64]{1,2,0:T(8,128)} fusion(bf16[64,128,1]{2,0,1:T(8,128)(2,1)} %copy.128, bf16[64,128,128]{2,0,1:T(8,128)(2,1)S(1)} %fusion.4, bf16[64,64,3,3]{1,0,3,2:T(8,128)(2,1)S(1)} %copy-done.6), kind=kOutput, calls=%fused_computation.19 | convolution fusion | flops 138412032 | bytes 6324224 | tf_op jit(solution)/shard_map/oi,iyx->oyx/dot_general | solution.py:43
  404.6 3.9 copy.127
  408.5 1.0 pad_maximum_fusion.14
  409.5 1.9 collective-permute-start.10
  411.5 5.6 %collective-permute-start.11 = (bf16[64,1,130]{2,0,1:T(8,128)(2,1)S(1)}, bf16[64,1,130]{2,0,1:T(8,128)(2,1)S(1)}, u32[]{:S(2)}, u32[]{:S(2)}) collective-permute-start(bf16[64,1,130]{2,0,1:T(8,128)(2,1)S(1)} %get-tuple-element.94), channel_id=1, source_target_pairs={{1,0},{2,1},{3,2},{4,3},{5,4},{6,5},{7,6},{8,7},{9,8},{10,9},{11,1... | collective-permute-start | bytes 49928 | tf_op jit(solution)/shard_map/ppermute | solution.py:18
  417.1 3.1 fusion.15
  420.2 5.7 %maximum_maximum_fusion = (bf16[64,129,130]{2,0,1:T(8,128)(2,1)S(1)}, bf16[64,129,130]{2,0,1:T(8,128)(2,1)S(1)}) fusion(bf16[64,128,1]{2,0,1:T(8,128)(2,1)S(1)} %copy-done.2, bf16[64,128,128]{2,0,1:T(8,128)(2,1)S(1)} %fusion.4, bf16[64,128,1]{2,0,1:T(8,128)(2,1)S(1)} %copy-done.3, bf16[64,1,130]{2,0,1:T(8,128)(2,1)S(1)} %collective-permute-done.10, ...), kind=kLoop, calls=%fused_computation.3 | loop fusion | flops 17172480 | bytes 6456320 | tf_op jit(solution)/shard_map/concatenate | solution.py:19
  425.9 2.9 fusion.17
  428.8 2.8 fusion.19
  431.6 2.7 fusion.21
  434.3 2.9 fusion.9
  437.1 2.6 fusion.11
  439.8 12.1 %fusion.23 = bf16[64,128,128]{2,0,1:T(8,128)(2,1)S(1)} fusion(f32[64]{0:T(128)S(1)} %copy-done.9, bf16[64,129,130]{2,0,1:T(8,128)(2,1)S(1)} %get-tuple-element.92, f32[128,128,64]{1,2,0:T(8,128)} %fusion.9, f32[128,128,64]{1,2,0:T(8,128)} %fusion.11, f32[128,128,64]{1,2,0:T(8,128)} %fusion.13, f32[128,128,64]{1,2,0:T(8,128)} %fusion.142, ...), kind=kOutput, calls=%fused_computation.30 | convolution fusion | flops 144703488 | bytes 37765632 | tf_op jit(solution)/shard_map/oi,iyx->oyx/dot_general | solution.py:43
  451.9 2.7 copy.132
  (51 shorter events, 5.7 us)
Async XLA Ops:
  0.6 13.7 %copy-start = (bf16[128,6]{0,1:T(8,128)(2,1)S(1)}, bf16[128,6]{0,1:T(8,128)(2,1)}, u32[]{:S(2)}) copy-start(bf16[128,6]{0,1:T(8,128)(2,1)} %param.10) | copy-start | bytes 4612
  4.0 19.9 %all-to-all-start.1 = ((bf16[128,2,6]{2,1,0:T(2,128)(2,1)}), bf16[128,2,6]{2,1,0:T(2,128)(2,1)S(1)}, u32[]{:S(2)}, u32[]{:S(2)}) async-start(bf16[128,2,6]{2,1,0:T(2,128)(2,1)} %broadcast_in_dim.23), calls=%async_computation.1 | async-start | bytes 131072 | tf_op jit(solution)/shard_map/all_to_all | solution.py:128
  24.0 62.0 %all-to-all-start.2 = ((bf16[128,2,6]{2,1,0:T(2,128)(2,1)}), bf16[128,2,6]{2,1,0:T(2,128)(2,1)S(1)}, u32[]{:S(2)}, u32[]{:S(2)}) async-start(bf16[128,2,6]{2,1,0:T(2,128)(2,1)} %bitcast.5), calls=%async_computation.2 | async-start | bytes 131072 | tf_op jit(solution)/shard_map/all_to_all | solution.py:121
  86.0 10.8 %copy-start.5 = (f32[6,9,9]{2,0,1:T(8,128)S(1)}, f32[6,9,9]{2,0,1:T(8,128)}, u32[]{:S(2)}) copy-start(f32[6,9,9]{2,0,1:T(8,128)} %param.13) | copy-start | bytes 5836
  86.0 15.1 %copy-start.7 = (bf16[64,6,3,3]{0,3,2,1:T(4,128)(2,1)S(1)}, bf16[64,6,3,3]{0,3,2,1:T(4,128)(2,1)}, u32[]{:S(2)}) copy-start(bf16[64,6,3,3]{0,3,2,1:T(4,128)(2,1)} %param.14) | copy-start | bytes 20740
  86.0 166.5 %all-to-all-start = ((bf16[128,2,6,4096]{3,1,2,0:T(2,128)(2,1)}), bf16[128,2,6,4096]{3,1,2,0:T(2,128)(2,1)}, u32[]{:S(2)}, u32[]{:S(2)}) async-start(bf16[128,2,6,4096]{3,1,2,0:T(2,128)(2,1)} %copy.104), calls=%async_computation | async-start | bytes 25165824 | tf_op jit(solution)/shard_map/all_to_all | solution.py:114
  292.7 8.0 %collective-permute-start = (f32[6,128,4]{2,0,1:T(8,128)S(1)}, f32[6,128,4]{2,0,1:T(8,128)S(1)}, u32[]{:S(2)}, u32[]{:S(2)}) collective-permute-start(f32[6,128,4]{2,0,1:T(8,128)S(1)} %get-tuple-element.105), channel_id=1, source_target_pairs={{0,16},{16,32},{32,48},{48,64},{64,80},{80,96},{96,112},{1,17},{17... | collective-permute-start | bytes 36872 | tf_op jit(solution)/shard_map/ppermute | solution.py:17
  294.6 10.8 %collective-permute-start.1 = (f32[6,128,4]{2,0,1:T(8,128)S(1)}, f32[6,128,4]{2,0,1:T(8,128)S(1)}, u32[]{:S(2)}, u32[]{:S(2)}) collective-permute-start(f32[6,128,4]{2,0,1:T(8,128)S(1)} %get-tuple-element.106), channel_id=1, source_target_pairs={{16,0},{32,16},{48,32},{64,48},{80,64},{96,80},{112,96},{17,1},{33... | collective-permute-start | bytes 36872 | tf_op jit(solution)/shard_map/ppermute | solution.py:18
  305.5 11.4 %collective-permute-start.2 = (f32[6,4,136]{2,0,1:T(8,128)S(1)}, f32[6,4,136]{2,0,1:T(8,128)S(1)}, u32[]{:S(2)}, u32[]{:S(2)}) collective-permute-start(f32[6,4,136]{2,0,1:T(8,128)S(1)} %get-tuple-element.99), channel_id=1, source_target_pairs={{0,1},{1,2},{2,3},{3,4},{4,5},{5,6},{6,7},{7,8},{8,9},{9,10},{10,1... | collective-permute-start | bytes 39176 | tf_op jit(solution)/shard_map/ppermute | solution.py:17
  314.8 4.7 %collective-permute-start.3 = (f32[6,4,136]{2,0,1:T(8,128)S(1)}, f32[6,4,136]{2,0,1:T(8,128)S(1)}, u32[]{:S(2)}, u32[]{:S(2)}) collective-permute-start(f32[6,4,136]{2,0,1:T(8,128)S(1)} %get-tuple-element.100), channel_id=1, source_target_pairs={{1,0},{2,1},{3,2},{4,3},{5,4},{6,5},{7,6},{8,7},{9,8},{10,9},{11,1... | collective-permute-start | bytes 39176 | tf_op jit(solution)/shard_map/ppermute | solution.py:18
  316.9 1.0 copy-start.4
  334.3 6.4 %collective-permute-start.4 = (bf16[6,128,1]{2,0,1:T(8,128)(2,1)S(1)}, bf16[6,128,1]{2,0,1:T(8,128)(2,1)S(1)}, u32[]{:S(2)}, u32[]{:S(2)}) collective-permute-start(bf16[6,128,1]{2,0,1:T(8,128)(2,1)S(1)} %get-tuple-element.109), channel_id=1, source_target_pairs={{0,16},{16,32},{32,48},{48,64},{64,80},{80,96},{96,112},{1,17},{17... | collective-permute-start | bytes 4616 | tf_op jit(solution)/shard_map/ppermute | solution.py:17
  337.3 7.7 %collective-permute-start.5 = (bf16[6,128,1]{2,0,1:T(8,128)(2,1)S(1)}, bf16[6,128,1]{2,0,1:T(8,128)(2,1)S(1)}, u32[]{:S(2)}, u32[]{:S(2)}) collective-permute-start(bf16[6,128,1]{2,0,1:T(8,128)(2,1)S(1)} %get-tuple-element.110), channel_id=1, source_target_pairs={{16,0},{32,16},{48,32},{64,48},{80,64},{96,80},{112,96},{17,1},{33... | collective-permute-start | bytes 4616 | tf_op jit(solution)/shard_map/ppermute | solution.py:18
  345.0 9.1 %collective-permute-start.6 = (bf16[6,1,130]{2,0,1:T(8,128)(2,1)S(1)}, bf16[6,1,130]{2,0,1:T(8,128)(2,1)S(1)}, u32[]{:S(2)}, u32[]{:S(2)}) collective-permute-start(bf16[6,1,130]{2,0,1:T(8,128)(2,1)S(1)} %get-tuple-element.103), channel_id=1, source_target_pairs={{0,1},{1,2},{2,3},{3,4},{4,5},{5,6},{6,7},{7,8},{8,9},{9,10},{10,1... | collective-permute-start | bytes 4688 | tf_op jit(solution)/shard_map/ppermute | solution.py:17
  347.0 7.2 %collective-permute-start.7 = (bf16[6,1,130]{2,0,1:T(8,128)(2,1)S(1)}, bf16[6,1,130]{2,0,1:T(8,128)(2,1)S(1)}, u32[]{:S(2)}, u32[]{:S(2)}) collective-permute-start(bf16[6,1,130]{2,0,1:T(8,128)(2,1)S(1)} %get-tuple-element.104), channel_id=1, source_target_pairs={{1,0},{2,1},{3,2},{4,3},{5,4},{6,5},{7,6},{8,7},{9,8},{10,9},{11,1... | collective-permute-start | bytes 4688 | tf_op jit(solution)/shard_map/ppermute | solution.py:18
  362.8 5.4 %copy-start.8 = (f32[64]{0:T(128)S(1)}, f32[64]{0:T(128)}, u32[]{:S(2)}) copy-start(f32[64]{0:T(128)} %param.15) | copy-start | bytes 772
  376.9 8.5 %copy-start.6 = (bf16[64,64,3,3]{1,0,3,2:T(8,128)(2,1)S(1)}, bf16[64,64,3,3]{1,0,3,2:T(8,128)(2,1)}, u32[]{:S(2)}) copy-start(bf16[64,64,3,3]{1,0,3,2:T(8,128)(2,1)} %param.16) | copy-start | bytes 221188
  383.6 12.1 %collective-permute-start.9 = (bf16[64,128,1]{1,0,2:T(8,128)(2,1)S(1)}, bf16[64,128,1]{1,0,2:T(8,128)(2,1)S(1)}, u32[]{:S(2)}, u32[]{:S(2)}) collective-permute-start(bf16[64,128,1]{1,0,2:T(8,128)(2,1)S(1)} %copy.126), channel_id=1, source_target_pairs={{16,0},{32,16},{48,32},{64,48},{80,64},{96,80},{112,96},{17,1},{33... | collective-permute-start | bytes 49160 | tf_op jit(solution)/shard_map/ppermute | solution.py:18
  391.8 12.8 %collective-permute-start.8 = (bf16[64,128,1]{1,0,2:T(8,128)(2,1)S(1)}, bf16[64,128,1]{1,0,2:T(8,128)(2,1)S(1)}, u32[]{:S(2)}, u32[]{:S(2)}) collective-permute-start(bf16[64,128,1]{1,0,2:T(8,128)(2,1)S(1)} %copy.125), channel_id=1, source_target_pairs={{0,16},{16,32},{32,48},{48,64},{64,80},{80,96},{96,112},{1,17},{17... | collective-permute-start | bytes 49160 | tf_op jit(solution)/shard_map/ppermute | solution.py:17
  408.5 8.6 %copy-start.3 = (bf16[64,128,1]{2,0,1:T(8,128)(2,1)S(1)}, bf16[64,128,1]{2,0,1:T(8,128)(2,1)}, u32[]{:S(2)}) copy-start(bf16[64,128,1]{2,0,1:T(8,128)(2,1)} %copy.127) | copy-start | bytes 49156
  409.5 10.7 %collective-permute-start.10 = (bf16[64,1,130]{2,0,1:T(8,128)(2,1)S(1)}, bf16[64,1,130]{2,0,1:T(8,128)(2,1)S(1)}, u32[]{:S(2)}, u32[]{:S(2)}) collective-permute-start(bf16[64,1,130]{2,0,1:T(8,128)(2,1)S(1)} %get-tuple-element.93), channel_id=1, source_target_pairs={{0,1},{1,2},{2,3},{3,4},{4,5},{5,6},{6,7},{7,8},{8,9},{9,10},{10,1... | collective-permute-start | bytes 49928 | tf_op jit(solution)/shard_map/ppermute | solution.py:17
  411.5 8.7 %copy-start.2 = (bf16[64,128,1]{2,0,1:T(8,128)(2,1)S(1)}, bf16[64,128,1]{2,0,1:T(8,128)(2,1)}, u32[]{:S(2)}) copy-start(bf16[64,128,1]{2,0,1:T(8,128)(2,1)} %copy.128) | copy-start | bytes 49156
  411.5 8.7 %collective-permute-start.11 = (bf16[64,1,130]{2,0,1:T(8,128)(2,1)S(1)}, bf16[64,1,130]{2,0,1:T(8,128)(2,1)S(1)}, u32[]{:S(2)}, u32[]{:S(2)}) collective-permute-start(bf16[64,1,130]{2,0,1:T(8,128)(2,1)S(1)} %get-tuple-element.94), channel_id=1, source_target_pairs={{1,0},{2,1},{3,2},{4,3},{5,4},{6,5},{7,6},{8,7},{9,8},{10,9},{11,1... | collective-permute-start | bytes 49928 | tf_op jit(solution)/shard_map/ppermute | solution.py:18
  437.1 2.7 copy-start.9
  439.8 14.8 %copy-start.1 = (bf16[128,6]{0,1:T(8,128)(2,1)S(1)}, bf16[128,6]{0,1:T(8,128)(2,1)}, u32[]{:S(2)}) copy-start(bf16[128,6]{0,1:T(8,128)(2,1)} %param.10) | copy-start | bytes 4612
where the time goes:
time: 462 us; the launch traced here: 455 us
  waiting for transfers between devices  162 us (35%)
  local copies, waits for them, and re-layouts  115 us (25%)
  matrix products  78.6 us (17%)
  starting transfers between devices  74.5 us (16%)
  other arithmetic  22.9 us (5%)
    all_to_all x1, waiting for transfers between devices, body(): lax.all_to_all(sent_tiles.reshape(devices, capacity, band_count, pixel_ar...  151 us
    dot_general x18, matrix products, conv_three(): jnp.einsum('oi,iyx->oyx', weight[:, :, row_shift, col_shift], padded[:, r...  61.3 us
    reshape x2, local copies, waits for them, and re-layouts, body(): sent_tiles.reshape(devices, capacity, band_count, pixel_area)  43 us
    ppermute x6, starting transfers between devices, extended(): before = lax.ppermute(last, axis, up)  21.9 us
    ppermute x6, starting transfers between devices, extended(): after = lax.ppermute(first, axis, down)  21.7 us
    reshape x1, local copies, waits for them, and re-layouts, accumulate(): flat_tiles = got_tiles.reshape(-1, band_count, pixel_area)  19 us
    convert_element_type x1, other arithmetic, body(): psf_image = psf_apply(padded, psf_kernel).astype(jnp.bfloat16)  13.8 us
    unnamed x24, local copies, waits for them, and re-layouts  13.3 us
  transfers between devices with their start and end apart: 15, of which 5 were waited for; matrix products, arithmetic and copies ran while one was open for 19% of the time, Pallas kernels for 0%

commit v1 on v0

v1 whole, which is shorter than its diff:
```python
import functools

import jax
import jax.numpy as jnp
from jax import lax
from jax.experimental import pallas as pl
from jax.experimental.pallas import tpu as pltpu
from jax.sharding import PartitionSpec as P

MESH = pl.DeviceIdType.MESH
F32 = jnp.float32
BF16 = jnp.bfloat16

NB = 6
HALF = 2048
WIDE = HALF + 128
ORDER = (0, 2, 4, 1, 3, 5)
MEMBERS = ((2, 0), (2, 1), (1, 0), (3, 0), (1, 1), (3, 1), (0, 1))
AROUND = ((-1, 0), (1, 0), (0, -1), (0, 1), (-1, -1), (-1, 1), (1, -1), (1, 1))


def exchange_kernel(
    tiles_hbm,
    wt_ref,
    own_ref,
    cell_ref,
    img_ref,
    halo_ref,
    tin,
    sel,
    meta,
    metar,
    send_a,
    send_b,
    recv_a,
    recv_b,
    st2,
    rcv2,
    st3,
    rcv3,
    tbuf,
    hsend,
    hrecv,
    tin_sem,
    self_sem,
    s1_send,
    s1_recv,
    s2_send,
    s2_recv,
    s3_send,
    s3_recv,
    h_send,
    h_recv,
):
    ix = lax.axis_index("skyx")
    iy = lax.axis_index("skyy")
    core = ix % 2
    q = (ix // 2, iy % 4, iy // 4)

    def device(axis, step, flip):
        r = list(q)
        if step:
            r[axis] = (r[axis] + step) % 4
        c = (core + flip) % 2 if flip else core
        return (r[0] * 2 + c, r[2] * 4 + r[1])

    def around(dy, dx):
        return ((ix + dx + 8) % 8, (iy + dy + 16) % 16)

    barrier = pltpu.get_barrier_semaphore()
    peers = [device(0, 0, 1)]
    for axis in range(3):
        for step, flip in MEMBERS[:6]:
            peers.append(device(axis, step, flip))
    for dy, dx in AROUND:
        peers.append(around(dy, dx))
    for peer in peers:
        pl.semaphore_signal(barrier, inc=1, device_id=peer, device_id_type=MESH)

    tin_copies = {}
    for b in ORDER:
        tin_copies[b] = pltpu.make_async_copy(tiles_hbm.at[b], tin.at[b], tin_sem.at[b])
        tin_copies[b].start()

    own = own_ref[...]
    ox, oy = own // 16, own % 16
    oq = (ox // 2, oy % 4, oy // 4)
    oc = ox % 2
    ownf = jnp.broadcast_to(own.astype(F32), (128, 128))
    same = ownf == ownf.T
    earlier = lax.broadcasted_iota(jnp.int32, (128, 128), 0) < lax.broadcasted_iota(
        jnp.int32, (128, 128), 1
    )
    rank = jnp.sum(jnp.where(same & earlier, 1.0, 0.0), axis=0, keepdims=True).astype(jnp.int32)
    rows = lax.broadcasted_iota(jnp.int32, (256, 128), 0)
    for p in range(3):
        slot = (oq[p] * 2 + oc) * 32 + (oq[(p + 1) % 3] * 4 + oq[(p + 2) % 3]) * 2 + rank
        sel[p] = jnp.where(rows == slot, 1.0, 0.0).astype(BF16)
    meta[...] = jnp.zeros((128, 128), F32)
    meta[0:6, :] = wt_ref[...].astype(F32)
    meta[6:7, :] = cell_ref[...].astype(F32) + 1.0

    s1 = {}

    def stage1_refs(b):
        p, k = b // 2, b % 2
        return (send_a.at[p], recv_a.at[p]) if k == 0 else (send_b.at[p], recv_b.at[p])

    for n, b in enumerate(ORDER):
        p, k = b // 2, b % 2
        src, dst = stage1_refs(b)
        tin_copies[b].wait()

        def gather(c, carry, b=b, p=p, src=src):
            at = pl.ds(pl.multiple_of(c * 512, 512), 512)
            src[:, at] = jnp.dot(sel[p], tin[b, :, at], preferred_element_type=F32).astype(BF16)
            return carry

        lax.fori_loop(0, 8, gather, 0)
        if k == 0:
            src[:, 4096:4224] = lax.dot_general(
                sel[p],
                meta[...].astype(BF16),
                (((1,), (1,)), ((), ())),
                preferred_element_type=F32,
            ).astype(BF16)
        if n == 0:
            pl.semaphore_wait(barrier, len(peers))
        mine = q[p] * 2 + core
        mine_rows = pl.ds(pl.multiple_of(mine * 32, 32), 32)
        own_copy = pltpu.make_async_copy(src.at[mine_rows], dst.at[mine_rows], self_sem.at[b])
        own_copy.start()
        copies = [own_copy]
        for m, (step, flip) in enumerate(MEMBERS):
            there = ((q[p] + step) % 4) * 2 + (core + flip) % 2
            copy = pltpu.make_async_remote_copy(
                src_ref=src.at[pl.ds(pl.multiple_of(there * 32, 32), 32)],
                dst_ref=dst.at[mine_rows],
                send_sem=s1_send.at[b, m],
                recv_sem=s1_recv.at[b, m],
                device_id=device(p, step, flip),
                device_id_type=MESH,
            )
            copy.start()
            copies.append(copy)
        s1[b] = copies

    s2, s3 = {}, {}

    def reduce_tiles(b):
        p, k = b // 2, b % 2
        src, dst = stage1_refs(b)
        s1[b][0].wait()
        for copy in s1[b][1:]:
            copy.wait_recv()
        if k == 0:
            metar[p] = dst[:, 4096:4224].astype(F32).T[0:8, :]
        w = metar[p, b : b + 1, :]
        code = metar[p, 6:7, :].astype(jnp.int32)
        row = lax.broadcasted_iota(jnp.int32, (128, 256), 0)
        col = lax.broadcasted_iota(jnp.int32, (128, 256), 1)
        hit = ((col % 32) // 2 == row // 8) & (code == row % 4 + 1)
        upper = (row // 4) % 2 == 0
        both = jnp.where(hit, jnp.broadcast_to(w, (128, 256)), 0.0)
        c0 = jnp.where(upper, both, 0.0).astype(BF16)
        c1 = jnp.where(upper, 0.0, both).astype(BF16)
        st2[b, :, HALF:WIDE] = jnp.broadcast_to(
            jnp.sum(both, axis=1, keepdims=True), (128, 128)
        )

        def reduce(c, carry):
            lo = pl.ds(pl.multiple_of(c * 512, 512), 512)
            hi = pl.ds(pl.multiple_of(c * 512 + HALF, 512), 512)
            st2[b, :, lo] = jnp.dot(c0, dst[:, lo], preferred_element_type=F32) + jnp.dot(
                c1, dst[:, hi], preferred_element_type=F32
            )
            return carry

        lax.fori_loop(0, 4, reduce, 0)
        axis = (p + 1) % 3
        copies = []
        for step in (2, 1, 3):
            there = (q[axis] + step) % 4
            copy = pltpu.make_async_remote_copy(
                src_ref=st2.at[b, pl.ds(pl.multiple_of(there * 32, 32), 32)],
                dst_ref=rcv2.at[b, step - 1],
                send_sem=s2_send.at[b, step - 1],
                recv_sem=s2_recv.at[b, step - 1],
                device_id=device(axis, step, 0),
                device_id_type=MESH,
            )
            copy.start()
            copies.append(copy)
        s2[b] = copies

    def second(b):
        p = b // 2
        axis = (p + 1) % 3
        for copy in s2[b]:
            copy.wait_recv()
        at = pl.ds(pl.multiple_of(q[axis] * 32, 32), 32)
        st3[b] = (st2[b, at, :] + rcv2[b, 0]) + (rcv2[b, 1] + rcv2[b, 2])
        axis = (p + 2) % 3
        copies = []
        for step in (2, 1, 3):
            there = (q[axis] + step) % 4
            copy = pltpu.make_async_remote_copy(
                src_ref=st3.at[b, pl.ds(pl.multiple_of(there * 8, 8), 8)],
                dst_ref=rcv3.at[b, step - 1],
                send_sem=s3_send.at[b, step - 1],
                recv_sem=s3_recv.at[b, step - 1],
                device_id=device(axis, step, 0),
                device_id_type=MESH,
            )
            copy.start()
            copies.append(copy)
        s3[b] = copies

    left_half = lax.broadcasted_iota(jnp.int32, (16, 128), 1) < 64

    def third(b):
        p = b // 2
        axis = (p + 2) % 3
        for copy in s3[b]:
            copy.wait_recv()
        at = pl.ds(pl.multiple_of(q[axis] * 8, 8), 8)
        total = (st3[b, at, :] + rcv3[b, 0]) + (rcv3[b, 1] + rcv3[b, 2])
        scale = 1.0 / (1.0 + total[:, HALF:WIDE])
        for j in range(16):
            tbuf[pl.ds(j, 8, stride=16), :] = total[:, 128 * j : 128 * j + 128] * scale
        for h in range(2):
            for cy in range(2):
                s = h * 4 + cy * 2
                a = tbuf[16 * s : 16 * s + 16, :]
                c = tbuf[16 * s + 16 : 16 * s + 32, :]
                y0 = 64 * cy + 32 * h
                img_ref[b, pl.ds(y0, 16, stride=2), :] = jnp.where(
                    left_half, a, pltpu.roll(c, 64, 1)
                )
                img_ref[b, pl.ds(y0 + 1, 16, stride=2), :] = jnp.where(
                    left_half, pltpu.roll(a, 64, 1), c
                )
        hsend[0, b] = img_ref[b, 0:8, :]
        hsend[1, b] = img_ref[b, 120:128, :]
        turned = img_ref[b].T
        hsend[2, b] = turned[0:8, :]
        hsend[3, b] = turned[120:128, :]

    todo = []
    for n in range(6 + 4):
        if n < 6:
            todo.append((reduce_tiles, n))
        if 0 <= n - 2 < 6:
            todo.append((second, n - 2))
        if 0 <= n - 4 < 6:
            todo.append((third, n - 4))
    for step_fn, n in todo:
        step_fn(ORDER[n])

    halo = []
    for n, (dy, dx) in enumerate(AROUND):
        which = 0 if dy < 0 else 1 if dy > 0 else 2 if dx < 0 else 3
        copy = pltpu.make_async_remote_copy(
            src_ref=hsend.at[which],
            dst_ref=hrecv.at[n],
            send_sem=h_send.at[n],
            recv_sem=h_recv.at[n],
            device_id=around(dy, dx),
            device_id_type=MESH,
        )
        copy.start()
        halo.append(copy)
    for b in ORDER:
        for copy in s1[b][1:] + s2[b] + s3[b]:
            copy.wait_send()
    for n, copy in enumerate(halo):
        copy.wait_recv()
        halo_ref[n] = hrecv[n]
    for copy in halo:
        copy.wait_send()


def exchange(tiles, weights, owners, cells):
    vmem = pl.BlockSpec(memory_space=pltpu.VMEM)
    dma = pltpu.SemaphoreType.DMA
    return pl.pallas_call(
        exchange_kernel,
        out_shape=(
            jax.ShapeDtypeStruct((NB, 128, 128), F32),
            jax.ShapeDtypeStruct((8, NB, 8, 128), F32),
        ),
        in_specs=[pl.BlockSpec(memory_space=pl.ANY), vmem, vmem, vmem],
        out_specs=(vmem, vmem),
        scratch_shapes=[
            pltpu.VMEM((NB, 128, 4096), BF16),
            pltpu.VMEM((3, 256, 128), BF16),
            pltpu.VMEM((128, 128), F32),
            pltpu.VMEM((3, 8, 256), F32),
            pltpu.VMEM((3, 256, 4224), BF16),
            pltpu.VMEM((3, 256, 4096), BF16),
            pltpu.VMEM((3, 256, 4224), BF16),
            pltpu.VMEM((3, 256, 4096), BF16),
            pltpu.VMEM((NB, 128, WIDE), F32),
            pltpu.VMEM((NB, 3, 32, WIDE), F32),
            pltpu.VMEM((NB, 32, WIDE), F32),
            pltpu.VMEM((NB, 3, 8, WIDE), F32),
            pltpu.VMEM((128, 128), F32),
            pltpu.VMEM((4, NB, 8, 128), F32),
            pltpu.VMEM((8, NB, 8, 128), F32),
            dma((NB,)),
            dma((NB,)),
            dma((NB, 7)),
            dma((NB, 7)),
            dma((NB, 3)),
            dma((NB, 3)),
            dma((NB, 3)),
            dma((NB, 3)),
            dma((8,)),
            dma((8,)),
        ],
        compiler_params=pltpu.CompilerParams(
            collective_id=0, has_side_effects=True, vmem_limit_bytes=60 * 1024 * 1024
        ),
        name="tile_exchange",
    )(tiles, weights, owners, cells)


def detect_kernel(
    taps_ref,
    img_ref,
    halo_ref,
    w1_ref,
    b1_ref,
    w2_ref,
    b2_ref,
    psf_ref,
    det_ref,
    ext,
    shifted,
    psf,
    taps3,
    hidden,
    turned,
):
    ix = lax.axis_index("skyx")
    iy = lax.axis_index("skyy")
    top, bottom = (iy > 0).astype(F32), (iy < 15).astype(F32)
    left, right = (ix > 0).astype(F32), (ix < 7).astype(F32)
    lane = lax.broadcasted_iota(jnp.int32, (8, 128), 1)
    side = jnp.where(lane < 64, right, left)
    taps3[...] = jnp.zeros_like(taps3)

    for b in range(NB):
        ext[b, 0, 8:136, :] = img_ref[b]
        ext[b, 0, 0:8, :] = halo_ref[1, b] * top
        ext[b, 0, 136:144, :] = halo_ref[0, b] * bottom
        columns = jnp.concatenate(
            [halo_ref[2, b] * right, jnp.zeros((112, 128), F32), halo_ref[3, b] * left], axis=0
        )
        ext[b, 1, 8:136, :] = columns.T
        ext[b, 1, 0:8, :] = jnp.where(lane < 64, halo_ref[6, b], halo_ref[7, b]) * (top * side)
        ext[b, 1, 136:144, :] = jnp.where(lane < 64, halo_ref[4, b], halo_ref[5, b]) * (
            bottom * side
        )

    def ring(x0, x1, by):
        n = x0.shape[0]
        at = lax.broadcasted_iota(jnp.int32, (n, 128), 1)
        r0, r1 = pltpu.roll(x0, (-by) % 128, 1), pltpu.roll(x1, (-by) % 128, 1)
        wrapped = at >= 128 - by if by > 0 else at < -by
        return jnp.where(wrapped, r1, r0), jnp.where(wrapped, r0, r1)

    def band(b, carry):
        x0, x1 = ext[b, 0], ext[b, 1]
        for j in range(9):
            if j == 4:
                shifted[j, 0], shifted[j, 1] = x0, x1
            else:
                shifted[j, 0], shifted[j, 1] = ring(x0, x1, j - 4)

        def block(start, size):
            acc = [jnp.zeros((size, 128), F32), jnp.zeros((size, 128), F32)]
            for i in range(9):
                for j in range(9):
                    tap = taps_ref[b * 81 + i * 9 + j]
                    for t in range(2):
                        acc[t] = acc[t] + tap * shifted[j, t, pl.ds(start + i, size), :]
            at = lax.broadcasted_iota(jnp.int32, (size, 128), 0) + start
            keep = jnp.where(at < 4, top, jnp.where(at >= 132, bottom, 1.0))
            at_lane = lax.broadcasted_iota(jnp.int32, (size, 128), 1)
            beside = keep * jnp.where(at_lane < 64, right, left)
            v0 = acc[0].astype(BF16).astype(F32) * keep
            v1 = acc[1].astype(BF16).astype(F32) * beside
            psf[pl.ds(start, size), :] = v0
            for jj in range(3):
                s0, s1 = (v0, v1) if jj == 1 else ring(v0, v1, jj - 1)
                where = pl.ds(start * 24 + 8 * jj + b, size, stride=24)
                taps3[0, where, :] = s0
                taps3[1, where, :] = s1

        def blocks(n, inner):
            block(pl.multiple_of(n * 32, 32), 32)
            return inner

        lax.fori_loop(0, 4, blocks, 0)
        block(128, 8)
        psf_ref[b] = psf[4:132, :].astype(BF16)
        return carry

    lax.fori_loop(0, NB, band, 0)

    bias1 = jnp.broadcast_to(b1_ref[...], (64, 256))
    lanes = lax.broadcasted_iota(jnp.int32, (64, 256), 1)
    inside = jnp.where(lanes < 128, 1.0, jnp.where(lanes < 192, right, left))
    w1 = w1_ref[...]

    def first(n, carry):
        at = pl.ds(pl.multiple_of((n + 2) * 24, 8), 72)
        rhs = jnp.concatenate([taps3[0, at, :], taps3[1, at, :]], axis=1).astype(BF16)
        v = jnp.dot(w1, rhs, preferred_element_type=F32) + bias1
        keep = jnp.where(n == 0, top, jnp.where(n == 129, bottom, 1.0))
        v = v / (1.0 + jnp.exp(-v))
        hidden[n] = (v * (inside * keep)).astype(BF16)
        return carry

    lax.fori_loop(0, 130, first, 0)

    bias2 = jnp.broadcast_to(b2_ref[...], (64, 128))
    w2 = w2_ref[...]
    at_lane = lax.broadcasted_iota(jnp.int32, (64, 128), 1)

    def group(g, carry):
        def row(yy, inner):
            y = g * 16 + yy
            rhs = hidden[pl.ds(y, 3)].reshape(192, 256)
            z = jnp.dot(w2, rhs, preferred_element_type=F32)
            before = pltpu.roll(
                jnp.where(at_lane == 127, z[0:64, 128:256], z[0:64, 0:128]), 1, 1
            )
            after = pltpu.roll(
                jnp.where(at_lane == 0, z[128:192, 128:256], z[128:192, 0:128]), 127, 1
            )
            turned[pl.ds(yy, 64, stride=16), :] = (before + z[64:128, 0:128]) + (after + bias2)
            return inner

        lax.fori_loop(0, 16, row, 0, unroll=4)
        det_ref[:, pl.ds(pl.multiple_of(g * 16, 16), 16), :] = (
            turned[...].reshape(64, 16, 128).astype(BF16)
        )
        return carry

    lax.fori_loop(0, 8, group, 0)


def detect(taps, image, halo, w1, b1, w2, b2):
    vmem = pl.BlockSpec(memory_space=pltpu.VMEM)
    return pl.pallas_call(
        detect_kernel,
        out_shape=(
            jax.ShapeDtypeStruct((NB, 128, 128), BF16),
            jax.ShapeDtypeStruct((64, 128, 128), BF16),
        ),
        in_specs=[pl.BlockSpec(memory_space=pltpu.SMEM)] + [vmem] * 6,
        out_specs=(vmem, vmem),
        scratch_shapes=[
            pltpu.VMEM((NB, 2, 144, 128), F32),
            pltpu.VMEM((9, 2, 144, 128), F32),
            pltpu.VMEM((136, 128), F32),
            pltpu.VMEM((2, 136 * 24, 128), F32),
            pltpu.VMEM((130, 64, 256), BF16),
            pltpu.VMEM((64 * 16, 128), F32),
        ],
        compiler_params=pltpu.CompilerParams(vmem_limit_bytes=48 * 1024 * 1024),
        name="detect",
    )(taps, image, halo, w1, b1, w2, b2)


def body(
    tiles,
    tile_weight,
    owners,
    cells,
    psf_kernel,
    conv1_weight,
    conv1_bias,
    conv2_weight,
    conv2_bias,
):
    image, halo = exchange(
        tiles.transpose(1, 0, 2),
        tile_weight.transpose(1, 0),
        owners.reshape(1, 128),
        cells.reshape(1, 128),
    )
    w1 = jnp.pad(conv1_weight.transpose(0, 2, 3, 1), ((0, 0), (0, 0), (0, 0), (0, 2)))
    w2 = conv2_weight.transpose(3, 0, 2, 1).reshape(192, 192)
    return detect(
        psf_kernel.reshape(-1),
        image,
        halo,
        w1.reshape(64, 72),
        conv1_bias[:, None],
        w2,
        conv2_bias[:, None],
    )


def solution(mesh):
    in_specs = (
        P(("skyx", "skyy"), None, None),
        P(("skyx", "skyy"), None),
        P(("skyx", "skyy"), None),
        P(("skyx", "skyy")),
        P(),
        P(),
        P(),
        P(),
        P(),
    )
    out_specs = (P(None, "skyy", "skyx"), P(None, "skyy", "skyx"))
    return jax.shard_map(body, mesh=mesh, in_specs=in_specs, out_specs=out_specs, check_vma=False)
```

time: 462 us -> 162 us (0.35)
  the two profiles are of different devices: /device:TPU:69 before, /device:TPU:1 now
where the time goes in v1:
time: 162 us
  Pallas kernels  155 us (96%)
  local copies, waits for them, and re-layouts  6.35 us (4%)
    pallas_call x1, Pallas kernels, exchange(): pl.pallas_call(exchange_kernel, out_shape=(jax.ShapeDtypeStruct((NB, 128,...  109 us
    pallas_call x1, Pallas kernels, detect(): pl.pallas_call(detect_kernel, out_shape=(jax.ShapeDtypeStruct((NB, 128, 1...  45.2 us
    unnamed x6, local copies, waits for them, and re-layouts  3.42 us

profile of v1, /device:TPU:1, one launch (start us, length us, event | category | flops | bytes accessed | tf_op | source)
XLA Modules:
  0.0 161.7 jit_solution(1506678462459192998)
XLA Ops:
  0.6 0.7 copy.21
  1.4 0.1 copy.18.w1_ref
  1.5 0.8 copy.19.b1_ref
  2.2 0.7 copy.20.b2_ref
  3.0 0.8 copy.15
  3.7 0.1 reshape.19.taps_ref
  3.9 1.0 copy.17
  4.9 0.2 reshape.23.w2_ref
  5.1 109.5 %tile_exchange.1 = (f32[6,128,128]{2,1,0:T(8,128)}, f32[8,6,8,128]{3,2,1,0:T(8,128)}) custom-call(bf16[6,128,4096]{2,1,0:T(8,128)(2,1)} %bitcast.9, bf16[6,128]{1,0:T(8,128)(2,1)} %bitcast.13, s32[1,128]{1,0:T(1,128)} %bitcast.16, s32[1,128]{1,0:T(1,128)} %bitcast.17), custom_call_target="tpu_custom_call" | custom-call | tf_op jit(solution)/shard_map/tile_exchange/pallas_call | solution.py:286
  114.6 0.0 copy-start
  114.6 1.0 copy-done
  115.6 0.0 copy-start.1
  115.6 0.9 copy-done.1
  116.5 45.2 %detect.1 = (bf16[6,128,128]{2,1,0:T(8,128)(2,1)}, bf16[64,128,128]{2,1,0:T(8,128)(2,1)}) custom-call(f32[486]{0:T(512)S(1)} %reshape.19.taps_ref, f32[6,128,128]{2,1,0:T(8,128)S(1)} %copy-done, f32[8,6,8,128]{3,2,1,0:T(8,128)S(1)} %copy-done.1, bf16[64,72]{1,0:T(8,128)(2,1)S(1)} %copy.18.w1_ref, f32[64,1]{1,0:T(8,128)S(1)} %copy.19.b1_ref, ...), custom_call_target="tpu_custom_call" | custom-call | tf_op jit(solution)/shard_map/detect/pallas_call | solution.py:457
  (1 shorter events, 0.0 us)
Async XLA Ops:
  114.6 1.0 copy-start
  115.6 0.9 copy-start.1

commit v2 on v1

--- a/solution.py
+++ b/solution.py
@@ -24,8 +24,7 @@
     wt_ref,
     own_ref,
     cell_ref,
-    img_ref,
-    halo_ref,
+    out_ref,
     tin,
     sel,
     meta,
@@ -234,17 +233,20 @@
                 a = tbuf[16 * s : 16 * s + 16, :]
                 c = tbuf[16 * s + 16 : 16 * s + 32, :]
                 y0 = 64 * cy + 32 * h
-                img_ref[b, pl.ds(y0, 16, stride=2), :] = jnp.where(
+                out_ref[pl.ds(128 * b + y0, 16, stride=2), :] = jnp.where(
                     left_half, a, pltpu.roll(c, 64, 1)
                 )
-                img_ref[b, pl.ds(y0 + 1, 16, stride=2), :] = jnp.where(
+                out_ref[pl.ds(128 * b + y0 + 1, 16, stride=2), :] = jnp.where(
                     left_half, pltpu.roll(a, 64, 1), c
                 )
-        hsend[0, b] = img_ref[b, 0:8, :]
-        hsend[1, b] = img_ref[b, 120:128, :]
-        turned = img_ref[b].T
+        r = 128 * b
+        hsend[0, b] = out_ref[r : r + 8, :]
+        hsend[1, b] = out_ref[r + 120 : r + 128, :]
+        turned = out_ref[r : r + 128, :].T
         hsend[2, b] = turned[0:8, :]
         hsend[3, b] = turned[120:128, :]
+        out_ref[1152 + 8 * b : 1160 + 8 * b, :] = turned[0:8, :]
+        out_ref[1200 + 8 * b : 1208 + 8 * b, :] = turned[120:128, :]
 
     todo = []
     for n in range(6 + 4):
@@ -275,7 +277,7 @@
             copy.wait_send()
     for n, copy in enumerate(halo):
         copy.wait_recv()
-        halo_ref[n] = hrecv[n]
+        out_ref[768 + 48 * n : 816 + 48 * n, :] = hrecv[n].reshape(48, 128)
     for copy in halo:
         copy.wait_send()
 
@@ -285,12 +287,9 @@
     dma = pltpu.SemaphoreType.DMA
     return pl.pallas_call(
         exchange_kernel,
-        out_shape=(
-            jax.ShapeDtypeStruct((NB, 128, 128), F32),
-            jax.ShapeDtypeStruct((8, NB, 8, 128), F32),
-        ),
+        out_shape=jax.ShapeDtypeStruct((1248, 128), F32),
         in_specs=[pl.BlockSpec(memory_space=pl.ANY), vmem, vmem, vmem],
-        out_specs=(vmem, vmem),
+        out_specs=vmem,
         scratch_shapes=[
             pltpu.VMEM((NB, 128, 4096), BF16),
             pltpu.VMEM((3, 256, 128), BF16),
@@ -327,8 +326,7 @@
 
 def detect_kernel(
     taps_ref,
-    img_ref,
-    halo_ref,
+    coadd_ref,
     w1_ref,
     b1_ref,
     w2_ref,
@@ -337,113 +335,201 @@
     det_ref,
     ext,
     shifted,
+    sides,
+    sides_t,
     psf,
     taps3,
+    edge3,
     hidden,
     turned,
+    small,
+    w2s,
 ):
     ix = lax.axis_index("skyx")
     iy = lax.axis_index("skyy")
     top, bottom = (iy > 0).astype(F32), (iy < 15).astype(F32)
     left, right = (ix > 0).astype(F32), (ix < 7).astype(F32)
-    lane = lax.broadcasted_iota(jnp.int32, (8, 128), 1)
-    side = jnp.where(lane < 64, right, left)
+
+    def halo(slot, b):
+        r = 768 + slot * 48 + b * 8
+        return coadd_ref[r : r + 8, :]
+
+    def lanes_of(n):
+        return lax.broadcasted_iota(jnp.int32, (n, 128), 1)
+
+    small[...] = jnp.zeros((128, 128), F32)
+    for b in range(NB):
+        for i in range(3):
+            small[pl.ds(i * 24 + b, 3, stride=8), 0:64] = w1_ref[b, i].astype(F32)
+    w1 = (small[...].T[0:64, 0:72] * 0.5).astype(BF16)
+    for j in range(3):
+        for i in range(3):
+            w2s[64 * j : 64 * j + 64, 64 * i : 64 * i + 64] = w2_ref[i, j]
+    small[0:1, 0:64] = b1_ref[...] * 0.5
+    small[1:2, 0:64] = b2_ref[...]
+    columns = small[...].T
+    bias1 = jnp.broadcast_to(columns[0:64, 0:1], (64, 256))
+    bias2 = jnp.broadcast_to(columns[0:64, 1:2], (64, 128))
+
+    pieces = []
+    for b in range(NB):
+        pieces += [
+            halo(3, b)[2:8] * left,
+            halo(8, b)[0:4],
+            halo(9, b)[4:8],
+            halo(2, b)[0:6] * right,
+        ]
+    pieces.append(jnp.zeros((8, 128), F32))
+    sides[8:136, :] = jnp.concatenate(pieces, axis=0).T
+    lane8 = lanes_of(8)
+    for r, mid, at_left, at_right, keep in ((0, 1, 7, 6, top), (136, 0, 5, 4, bottom)):
+        line = jnp.zeros((8, 128), F32)
+        for b in range(NB):
+            middle = halo(mid, b)
+            parts = (
+                (halo(at_left, b) * left, 122, 0, 6),
+                (middle, 0, 6, 4),
+                (middle, 124, 10, 4),
+                (halo(at_right, b) * right, 0, 14, 6),
+            )
+            for value, start, at, size in parts:
+                at = 20 * b + at
+                moved = pltpu.roll(value, (at - start) % 128, 1)
+                line = jnp.where((lane8 >= at) & (lane8 < at + size), moved, line)
+        sides[r : r + 8, :] = line * keep
+
+    for j in range(9):
+        shifted[j] = pltpu.roll(sides[...], (-j) % 128, 1) if j else sides[...]
+    owner_band = lane8 // 20
+
+    def edge_block(start, size):
+        acc = jnp.zeros((size, 128), F32)
+        for i in range(9):
+            for j in range(9):
+                tap = jnp.full((8, 128), taps_ref[i, 0, j], F32)
+                for b in range(1, NB):
+                    tap = jnp.where(owner_band == b, taps_ref[i, b, j], tap)
+                tap = jnp.broadcast_to(tap[0:1], (size, 128))
+                acc = acc + tap * shifted[j, start + i : start + i + size, :]
+        at = lax.broadcasted_iota(jnp.int32, (size, 128), 0) + start
+        keep = jnp.where(at < 4, top, jnp.where(at >= 132, bottom, 1.0))
+        keep = keep * jnp.where(lanes_of(size) % 20 < 10, left, right)
+        return acc.astype(BF16).astype(F32) * keep
+
+    sides[0:136, :] = edge_block(0, 136)
+
     taps3[...] = jnp.zeros_like(taps3)
-
     for b in range(NB):
-        ext[b, 0, 8:136, :] = img_ref[b]
-        ext[b, 0, 0:8, :] = halo_ref[1, b] * top
-        ext[b, 0, 136:144, :] = halo_ref[0, b] * bottom
-        columns = jnp.concatenate(
-            [halo_ref[2, b] * right, jnp.zeros((112, 128), F32), halo_ref[3, b] * left], axis=0
-        )
-        ext[b, 1, 8:136, :] = columns.T
-        ext[b, 1, 0:8, :] = jnp.where(lane < 64, halo_ref[6, b], halo_ref[7, b]) * (top * side)
-        ext[b, 1, 136:144, :] = jnp.where(lane < 64, halo_ref[4, b], halo_ref[5, b]) * (
-            bottom * side
-        )
-
-    def ring(x0, x1, by):
-        n = x0.shape[0]
-        at = lax.broadcasted_iota(jnp.int32, (n, 128), 1)
-        r0, r1 = pltpu.roll(x0, (-by) % 128, 1), pltpu.roll(x1, (-by) % 128, 1)
-        wrapped = at >= 128 - by if by > 0 else at < -by
-        return jnp.where(wrapped, r1, r0), jnp.where(wrapped, r0, r1)
+        ext[b, 8:136, :] = coadd_ref[128 * b : 128 * b + 128, :]
+        ext[b, 0:8, :] = halo(1, b) * top
+        ext[b, 136:144, :] = halo(0, b) * bottom
+    column = lanes_of(144)
 
     def band(b, carry):
-        x0, x1 = ext[b, 0], ext[b, 1]
+        near_left = pltpu.roll(shifted[0], 122 - 20 * b, 1)
+        near_right = pltpu.roll(shifted[0], 114 - 20 * b, 1)
+        x = ext[b]
         for j in range(9):
-            if j == 4:
-                shifted[j, 0], shifted[j, 1] = x0, x1
+            if j < 4:
+                moved = pltpu.roll(jnp.where(column >= 124 + j, near_left, x), 4 - j, 1)
+            elif j == 4:
+                moved = x
             else:
-                shifted[j, 0], shifted[j, 1] = ring(x0, x1, j - 4)
+                moved = pltpu.roll(jnp.where(column < j - 4, near_right, x), 132 - j, 1)
+            shifted[j + 1] = moved
 
         def block(start, size):
-            acc = [jnp.zeros((size, 128), F32), jnp.zeros((size, 128), F32)]
+            acc = jnp.zeros((size, 128), F32)
             for i in range(9):
                 for j in range(9):
-                    tap = taps_ref[b * 81 + i * 9 + j]
-                    for t in range(2):
-                        acc[t] = acc[t] + tap * shifted[j, t, pl.ds(start + i, size), :]
+                    acc = acc + taps_ref[i, b, j] * shifted[j + 1, start + i : start + i + size, :]
             at = lax.broadcasted_iota(jnp.int32, (size, 128), 0) + start
             keep = jnp.where(at < 4, top, jnp.where(at >= 132, bottom, 1.0))
-            at_lane = lax.broadcasted_iota(jnp.int32, (size, 128), 1)
-            beside = keep * jnp.where(at_lane < 64, right, left)
-            v0 = acc[0].astype(BF16).astype(F32) * keep
-            v1 = acc[1].astype(BF16).astype(F32) * beside
-            psf[pl.ds(start, size), :] = v0
-            for jj in range(3):
-                s0, s1 = (v0, v1) if jj == 1 else ring(v0, v1, jj - 1)
-                where = pl.ds(start * 24 + 8 * jj + b, size, stride=24)
-                taps3[0, where, :] = s0
-                taps3[1, where, :] = s1
-
-        def blocks(n, inner):
-            block(pl.multiple_of(n * 32, 32), 32)
-            return inner
-
-        lax.fori_loop(0, 4, blocks, 0)
-        block(128, 8)
+            v = acc.astype(BF16).astype(F32) * keep
+            psf[start : start + size, :] = v
+            lane = lanes_of(size)
+            edge = sides[start : start + size, :]
+            before = jnp.where(lane == 0, pltpu.roll(edge, 127 - 20 * b, 1), pltpu.roll(v, 1, 1))
+            after = jnp.where(
+                lane == 127, pltpu.roll(edge, 117 - 20 * b, 1), pltpu.roll(v, 127, 1)
+            )
+            for j, value in enumerate((before, v, after)):
+                taps3[pl.ds(start * 24 + 8 * j + b, size, stride=24), :] = value
+            edge = jnp.where(lane == 20 * b + 2, pltpu.roll(v, 20 * b + 2, 1), edge)
+            edge = jnp.where(lane == 20 * b + 9, pltpu.roll(v, 20 * b + 10, 1), edge)
+            sides[start : start + size, :] = edge
+
+        block(0, 72)
+        block(72, 64)
         psf_ref[b] = psf[4:132, :].astype(BF16)
         return carry
 
     lax.fori_loop(0, NB, band, 0)
 
-    bias1 = jnp.broadcast_to(b1_ref[...], (64, 256))
-    lanes = lax.broadcasted_iota(jnp.int32, (64, 256), 1)
-    inside = jnp.where(lanes < 128, 1.0, jnp.where(lanes < 192, right, left))
-    w1 = w1_ref[...]
+    def silu(u):
+        return u + u * jnp.tanh(u)
 
     def first(n, carry):
-        at = pl.ds(pl.multiple_of((n + 2) * 24, 8), 72)
-        rhs = jnp.concatenate([taps3[0, at, :], taps3[1, at, :]], axis=1).astype(BF16)
-        v = jnp.dot(w1, rhs, preferred_element_type=F32) + bias1
-        keep = jnp.where(n == 0, top, jnp.where(n == 129, bottom, 1.0))
-        v = v / (1.0 + jnp.exp(-v))
-        hidden[n] = (v * (inside * keep)).astype(BF16)
+        at0 = pl.ds(pl.multiple_of((2 * n + 2) * 24, 8), 72)
+        at1 = pl.ds(pl.multiple_of((2 * n + 3) * 24, 8), 72)
+        rhs = jnp.concatenate([taps3[at0, :], taps3[at1, :]], axis=1).astype(BF16)
+        v = silu(jnp.dot(w1, rhs, preferred_element_type=F32) + bias1)
+        hidden[2 * n] = v[:, 0:128].astype(BF16)
+        hidden[2 * n + 1] = v[:, 128:256].astype(BF16)
         return carry
 
-    lax.fori_loop(0, 130, first, 0)
-
-    bias2 = jnp.broadcast_to(b2_ref[...], (64, 128))
-    w2 = w2_ref[...]
-    at_lane = lax.broadcasted_iota(jnp.int32, (64, 128), 1)
+    lax.fori_loop(0, 65, first, 0, unroll=5)
+    hidden[0] = (hidden[0].astype(F32) * top).astype(BF16)
+    hidden[129] = (hidden[129].astype(F32) * bottom).astype(BF16)
+
+    sides_t[0] = sides[0:128, :].T
+    tail = jnp.concatenate([sides[128:136, :], jnp.zeros((120, 128), F32)], axis=0)
+    sides_t[1] = tail.T
+    edge3[...] = jnp.zeros_like(edge3)
+    at256 = lax.broadcasted_iota(jnp.int32, (64, 256), 1)
+    ends = jnp.where(at256 == 0, top, jnp.where(at256 == 129, bottom, 1.0))
+    beside = []
+    for side, (offset, keep) in enumerate(((0, left), (9, right))):
+        for t in range(2):
+            for j in range(3):
+                edge3[side, 8 * j : 8 * j + 6, 128 * t : 128 * t + 128] = sides_t[
+                    t, pl.ds(offset + j, 6, stride=20), :
+                ]
+        x = edge3[side]
+        rhs = jnp.concatenate([pltpu.roll(x, 256 - (2 + i), 1) for i in range(3)], axis=0)
+        v = silu(jnp.dot(w1, rhs.astype(BF16), preferred_element_type=F32) + bias1)
+        v = (v * (ends * keep)).astype(BF16).astype(F32)
+        rhs = jnp.concatenate(
+            [v[:, 0:128]] + [pltpu.roll(v, 256 - i, 1)[:, 0:128] for i in (1, 2)], axis=0
+        )
+        weight = w2s[0:64, :] if side == 0 else w2s[128:192, :]
+        beside.append(jnp.dot(weight, rhs.astype(BF16), preferred_element_type=F32))
+    small[0:64, :] = beside[0]
+    small[64:128, :] = beside[1]
+
+    w2 = w2s[...]
+    lane64 = lanes_of(64)
 
     def group(g, carry):
-        def row(yy, inner):
-            y = g * 16 + yy
-            rhs = hidden[pl.ds(y, 3)].reshape(192, 256)
+        def rows(n, inner):
+            y = g * 16 + 2 * n
+            rhs = jnp.concatenate(
+                [hidden[pl.ds(y, 3)].reshape(192, 128), hidden[pl.ds(y + 1, 3)].reshape(192, 128)],
+                axis=1,
+            )
             z = jnp.dot(w2, rhs, preferred_element_type=F32)
-            before = pltpu.roll(
-                jnp.where(at_lane == 127, z[0:64, 128:256], z[0:64, 0:128]), 1, 1
-            )
-            after = pltpu.roll(
-                jnp.where(at_lane == 0, z[128:192, 128:256], z[128:192, 0:128]), 127, 1
-            )
-            turned[pl.ds(yy, 64, stride=16), :] = (before + z[64:128, 0:128]) + (after + bias2)
+            for k in range(2):
+                c = slice(128 * k, 128 * k + 128)
+                near = pltpu.roll(small[0:64, :], 128 - (y + k), 1)
+                far = pltpu.roll(small[64:128, :], 127 - (y + k), 1)
+                before = jnp.where(lane64 == 0, near, pltpu.roll(z[0:64, c], 1, 1))
+                after = jnp.where(lane64 == 127, far, pltpu.roll(z[128:192, c], 127, 1))
+                turned[pl.ds(2 * n + k, 64, stride=16), :] = (before + z[64:128, c]) + (
+                    after + bias2
+                )
             return inner
 
-        lax.fori_loop(0, 16, row, 0, unroll=4)
+        lax.fori_loop(0, 8, rows, 0, unroll=4)
         det_ref[:, pl.ds(pl.multiple_of(g * 16, 16), 16), :] = (
             turned[...].reshape(64, 16, 128).astype(BF16)
         )
@@ -452,7 +538,7 @@
     lax.fori_loop(0, 8, group, 0)
 
 
-def detect(taps, image, halo, w1, b1, w2, b2):
+def detect(taps, coadd, w1, b1, w2, b2):
     vmem = pl.BlockSpec(memory_space=pltpu.VMEM)
     return pl.pallas_call(
         detect_kernel,
@@ -460,19 +546,24 @@
             jax.ShapeDtypeStruct((NB, 128, 128), BF16),
             jax.ShapeDtypeStruct((64, 128, 128), BF16),
         ),
-        in_specs=[pl.BlockSpec(memory_space=pltpu.SMEM)] + [vmem] * 6,
+        in_specs=[pl.BlockSpec(memory_space=pltpu.SMEM)] + [vmem] * 5,
         out_specs=(vmem, vmem),
         scratch_shapes=[
-            pltpu.VMEM((NB, 2, 144, 128), F32),
-            pltpu.VMEM((9, 2, 144, 128), F32),
+            pltpu.VMEM((NB, 144, 128), F32),
+            pltpu.VMEM((10, 144, 128), F32),
+            pltpu.VMEM((144, 128), F32),
+            pltpu.VMEM((2, 128, 128), F32),
             pltpu.VMEM((136, 128), F32),
-            pltpu.VMEM((2, 136 * 24, 128), F32),
-            pltpu.VMEM((130, 64, 256), BF16),
+            pltpu.VMEM((136 * 24, 128), F32),
+            pltpu.VMEM((2, 24, 256), F32),
+            pltpu.VMEM((130, 64, 128), BF16),
             pltpu.VMEM((64 * 16, 128), F32),
+            pltpu.VMEM((128, 128), F32),
+            pltpu.VMEM((192, 192), BF16),
         ],
         compiler_params=pltpu.CompilerParams(vmem_limit_bytes=48 * 1024 * 1024),
         name="detect",
-    )(taps, image, halo, w1, b1, w2, b2)
+    )(taps, coadd, w1, b1, w2, b2)
 
 
 def body(
@@ -486,22 +577,19 @@
     conv2_weight,
     conv2_bias,
 ):
-    image, halo = exchange(
+    coadd = exchange(
         tiles.transpose(1, 0, 2),
         tile_weight.transpose(1, 0),
         owners.reshape(1, 128),
         cells.reshape(1, 128),
     )
-    w1 = jnp.pad(conv1_weight.transpose(0, 2, 3, 1), ((0, 0), (0, 0), (0, 0), (0, 2)))
-    w2 = conv2_weight.transpose(3, 0, 2, 1).reshape(192, 192)
     return detect(
-        psf_kernel.reshape(-1),
-        image,
-        halo,
-        w1.reshape(64, 72),
-        conv1_bias[:, None],
-        w2,
-        conv2_bias[:, None],
+        psf_kernel.transpose(1, 0, 2),
+        coadd,
+        conv1_weight.transpose(1, 2, 3, 0),
+        conv1_bias.reshape(1, 64),
+        conv2_weight.transpose(2, 3, 0, 1),
+        conv2_bias.reshape(1, 64),
     )
 
 

time: 162 us -> 130 us (0.80)
  Pallas kernels: 155 us -> 128 us
  local copies, waits for them, and re-layouts: 6.35 us -> 1.1 us
    pallas_call x1, Pallas kernels: 45.2 us -> 18.7 us  [detect(): pl.pallas_call(detect_kernel, out_shape=(jax.ShapeDtypeStruct((NB, 128, 1...]
    unnamed x6 -> x12, local copies, waits for them, and re-layouts: 3.42 us -> 1.1 us
where the time goes in v2:
time: 130 us
  Pallas kernels  128 us (98%)
    pallas_call x1, Pallas kernels, exchange(): pl.pallas_call(exchange_kernel, out_shape=jax.ShapeDtypeStruct((1248, 128...  110 us
    pallas_call x1, Pallas kernels, detect(): pl.pallas_call(detect_kernel, out_shape=(jax.ShapeDtypeStruct((NB, 128, 1...  18.7 us

profile of v2, /device:TPU:1, one launch (start us, length us, event | category | flops | bytes accessed | tf_op | source)
XLA Modules:
  0.0 130.1 jit_solution(17422093689983931784)
XLA Ops:
  0.6 0.0 copy-start.5
  0.6 0.0 copy-start.1
  0.7 0.0 copy-start.4
  0.7 0.0 copy-start.3
  0.7 0.0 copy-start.2
  0.7 109.6 %tile_exchange.1.coadd_ref = f32[1248,128]{1,0:T(8,128)} custom-call(bf16[6,128,4096]{2,1,0:T(8,128)(2,1)} %bitcast.14, bf16[6,128]{1,0:T(8,128)(2,1)} %bitcast.15, s32[1,128]{1,0:T(1,128)} %bitcast.16, s32[1,128]{1,0:T(1,128)} %bitcast.17), custom_call_target="tpu_custom_call" | custom-call | tf_op jit(solution)/shard_map/tile_exchange/pallas_call | solution.py:288
  110.3 0.0 copy-done.5
  110.3 0.0 copy-done.1
  110.3 0.0 copy-done.4
  110.3 0.0 copy-done.3
  110.3 0.0 copy-done.2
  110.3 0.0 copy-start
  110.3 1.1 copy-done
  111.4 18.7 %detect.1 = (bf16[6,128,128]{2,1,0:T(8,128)(2,1)}, bf16[64,128,128]{2,1,0:T(8,128)(2,1)}) custom-call(f32[9,6,9]{2,1,0:T(8,128)S(1)} %bitcast.10, f32[1248,128]{1,0:T(8,128)S(1)} %copy-done, bf16[6,3,3,64]{3,2,1,0:T(4,128)(2,1)S(1)} %bitcast.11, f32[1,64]{1,0:T(1,128)S(1)} %bitcast.12, bf16[3,3,64,64]{3,2,1,0:T(8,128)(2,1)S(1)} %bitcast.9, f32[1,64]{1,0:T(1,128)S(1)} %bitcast.13), custom_call_target="tpu_custom_call" | custom-call | tf_op jit(solution)/shard_map/detect/pallas_call | solution.py:543
Async XLA Ops:
  0.6 109.7 %copy-start.5 = (f32[64]{0:T(128)S(1)}, f32[64]{0:T(128)}, u32[]{:S(2)}) copy-start(f32[64]{0:T(128)} %param.17) | copy-start | bytes 772
  0.6 109.7 %copy-start.1 = (bf16[64,64,3,3]{1,0,3,2:T(8,128)(2,1)S(1)}, bf16[64,64,3,3]{1,0,3,2:T(8,128)(2,1)}, u32[]{:S(2)}) copy-start(bf16[64,64,3,3]{1,0,3,2:T(8,128)(2,1)} %param.16) | copy-start | bytes 221188
  0.7 109.7 %copy-start.4 = (f32[64]{0:T(128)S(1)}, f32[64]{0:T(128)}, u32[]{:S(2)}) copy-start(f32[64]{0:T(128)} %param.15) | copy-start | bytes 772
  0.7 109.7 %copy-start.3 = (bf16[64,6,3,3]{0,3,2,1:T(4,128)(2,1)S(1)}, bf16[64,6,3,3]{0,3,2,1:T(4,128)(2,1)}, u32[]{:S(2)}) copy-start(bf16[64,6,3,3]{0,3,2,1:T(4,128)(2,1)} %param.14) | copy-start | bytes 20740
  0.7 109.7 %copy-start.2 = (f32[6,9,9]{2,0,1:T(8,128)S(1)}, f32[6,9,9]{2,0,1:T(8,128)}, u32[]{:S(2)}) copy-start(f32[6,9,9]{2,0,1:T(8,128)} %param.13) | copy-start | bytes 5836
  110.3 1.1 copy-start

commit v3 on v2

--- a/solution.py
+++ b/solution.py
@@ -13,7 +13,7 @@
 
 NB = 6
 HALF = 2048
-WIDE = HALF + 128
+QUARTER = 1024
 ORDER = (0, 2, 4, 1, 3, 5)
 MEMBERS = ((2, 0), (2, 1), (1, 0), (3, 0), (1, 1), (3, 1), (0, 1))
 AROUND = ((-1, 0), (1, 0), (0, -1), (0, 1), (-1, -1), (-1, 1), (1, -1), (1, 1))
@@ -33,10 +33,16 @@
     send_b,
     recv_a,
     recv_b,
+    acc2,
     st2,
+    st2m,
     rcv2,
+    rcv2m,
+    acc3,
     st3,
+    st3m,
     rcv3,
+    rcv3m,
     tbuf,
     hsend,
     hrecv,
@@ -146,6 +152,46 @@
 
     s2, s3 = {}, {}
 
+    def encode(values, denom, size):
+        top = jnp.max(jnp.abs(values), axis=1, keepdims=True)
+        some = top > 1e-30
+        inverse = jnp.where(some, 32767.0 / jnp.where(some, top, 1.0), 0.0)
+        codes = (values * inverse + 32768.5).astype(jnp.int32)
+        words = codes[:, :QUARTER] | (codes[:, QUARTER:] << 16)
+        lane = lax.broadcasted_iota(jnp.int32, (size, 128), 1)
+        return words, jnp.where(lane < 64, denom, top * (1.0 / 32767.0))
+
+    def decode(words, extra):
+        step = extra[:, 64:65]
+        low = (words & 65535).astype(F32) - 32768.0
+        high = lax.shift_right_logical(words, jnp.full_like(words, 16)).astype(F32) - 32768.0
+        return low * step, high * step
+
+    def gathered(own, own_denom, words, extras):
+        low, high, denom = own[:, :QUARTER], own[:, QUARTER:], own_denom
+        for k in range(3):
+            a, c = decode(words[k], extras[k])
+            low, high, denom = low + a, high + c, denom + extras[k][:, 0:1]
+        return low, high, denom
+
+    def pass_on(b, axis, size, words, extras, to_words, to_extras, send, recv):
+        copies = []
+        for step in (2, 1, 3):
+            there = (q[axis] + step) % 4
+            at = pl.ds(pl.multiple_of(there * size, size), size)
+            for n, (src, dst) in enumerate(((words, to_words), (extras, to_extras))):
+                copy = pltpu.make_async_remote_copy(
+                    src_ref=src.at[b, at],
+                    dst_ref=dst.at[b, step - 1],
+                    send_sem=send.at[b, step - 1, n],
+                    recv_sem=recv.at[b, step - 1, n],
+                    device_id=device(axis, step, 0),
+                    device_id_type=MESH,
+                )
+                copy.start()
+                copies.append(copy)
+        return copies
+
     def reduce_tiles(b):
         p, k = b // 2, b % 2
         src, dst = stage1_refs(b)
@@ -163,57 +209,30 @@
         both = jnp.where(hit, jnp.broadcast_to(w, (128, 256)), 0.0)
         c0 = jnp.where(upper, both, 0.0).astype(BF16)
         c1 = jnp.where(upper, 0.0, both).astype(BF16)
-        st2[b, :, HALF:WIDE] = jnp.broadcast_to(
-            jnp.sum(both, axis=1, keepdims=True), (128, 128)
-        )
+        denom = jnp.sum(both, axis=1, keepdims=True)
 
         def reduce(c, carry):
             lo = pl.ds(pl.multiple_of(c * 512, 512), 512)
             hi = pl.ds(pl.multiple_of(c * 512 + HALF, 512), 512)
-            st2[b, :, lo] = jnp.dot(c0, dst[:, lo], preferred_element_type=F32) + jnp.dot(
+            acc2[b, :, lo] = jnp.dot(c0, dst[:, lo], preferred_element_type=F32) + jnp.dot(
                 c1, dst[:, hi], preferred_element_type=F32
             )
             return carry
 
         lax.fori_loop(0, 4, reduce, 0)
-        axis = (p + 1) % 3
-        copies = []
-        for step in (2, 1, 3):
-            there = (q[axis] + step) % 4
-            copy = pltpu.make_async_remote_copy(
-                src_ref=st2.at[b, pl.ds(pl.multiple_of(there * 32, 32), 32)],
-                dst_ref=rcv2.at[b, step - 1],
-                send_sem=s2_send.at[b, step - 1],
-                recv_sem=s2_recv.at[b, step - 1],
-                device_id=device(axis, step, 0),
-                device_id_type=MESH,
-            )
-            copy.start()
-            copies.append(copy)
-        s2[b] = copies
+        st2[b], st2m[b] = encode(acc2[b], denom, 128)
+        s2[b] = pass_on(b, (p + 1) % 3, 32, st2, st2m, rcv2, rcv2m, s2_send, s2_recv)
 
     def second(b):
         p = b // 2
-        axis = (p + 1) % 3
         for copy in s2[b]:
             copy.wait_recv()
-        at = pl.ds(pl.multiple_of(q[axis] * 32, 32), 32)
-        st3[b] = (st2[b, at, :] + rcv2[b, 0]) + (rcv2[b, 1] + rcv2[b, 2])
-        axis = (p + 2) % 3
-        copies = []
-        for step in (2, 1, 3):
-            there = (q[axis] + step) % 4
-            copy = pltpu.make_async_remote_copy(
-                src_ref=st3.at[b, pl.ds(pl.multiple_of(there * 8, 8), 8)],
-                dst_ref=rcv3.at[b, step - 1],
-                send_sem=s3_send.at[b, step - 1],
-                recv_sem=s3_recv.at[b, step - 1],
-                device_id=device(axis, step, 0),
-                device_id_type=MESH,
-            )
-            copy.start()
-            copies.append(copy)
-        s3[b] = copies
+        at = pl.ds(pl.multiple_of(q[(p + 1) % 3] * 32, 32), 32)
+        low, high, denom = gathered(acc2[b, at, :], st2m[b, at, 0:1], rcv2[b], rcv2m[b])
+        acc3[b, :, :QUARTER] = low
+        acc3[b, :, QUARTER:] = high
+        st3[b], st3m[b] = encode(acc3[b], denom, 32)
+        s3[b] = pass_on(b, (p + 2) % 3, 8, st3, st3m, rcv3, rcv3m, s3_send, s3_recv)
 
     left_half = lax.broadcasted_iota(jnp.int32, (16, 128), 1) < 64
 
@@ -223,10 +242,12 @@
         for copy in s3[b]:
             copy.wait_recv()
         at = pl.ds(pl.multiple_of(q[axis] * 8, 8), 8)
-        total = (st3[b, at, :] + rcv3[b, 0]) + (rcv3[b, 1] + rcv3[b, 2])
-        scale = 1.0 / (1.0 + total[:, HALF:WIDE])
-        for j in range(16):
-            tbuf[pl.ds(j, 8, stride=16), :] = total[:, 128 * j : 128 * j + 128] * scale
+        low, high, denom = gathered(acc3[b, at, :], st3m[b, at, 0:1], rcv3[b], rcv3m[b])
+        scale = 1.0 / (1.0 + denom)
+        for j in range(8):
+            c = slice(128 * j, 128 * j + 128)
+            tbuf[pl.ds(j, 8, stride=16), :] = low[:, c] * scale
+            tbuf[pl.ds(j + 8, 8, stride=16), :] = high[:, c] * scale
         for h in range(2):
             for cy in range(2):
                 s = h * 4 + cy * 2
@@ -240,44 +261,51 @@
                     left_half, pltpu.roll(a, 64, 1), c
                 )
         r = 128 * b
-        hsend[0, b] = out_ref[r : r + 8, :]
-        hsend[1, b] = out_ref[r + 120 : r + 128, :]
+        n = ORDER.index(b)
+        hsend[0, n] = out_ref[r : r + 8, :]
+        hsend[1, n] = out_ref[r + 120 : r + 128, :]
         turned = out_ref[r : r + 128, :].T
-        hsend[2, b] = turned[0:8, :]
-        hsend[3, b] = turned[120:128, :]
+        hsend[2, n] = turned[0:8, :]
+        hsend[3, n] = turned[120:128, :]
         out_ref[1152 + 8 * b : 1160 + 8 * b, :] = turned[0:8, :]
         out_ref[1200 + 8 * b : 1208 + 8 * b, :] = turned[120:128, :]
 
-    todo = []
+    halo = []
+
+    def send_halo(group):
+        bands = pl.ds(3 * group, 3)
+        for n, (dy, dx) in enumerate(AROUND):
+            which = 0 if dy < 0 else 1 if dy > 0 else 2 if dx < 0 else 3
+            copy = pltpu.make_async_remote_copy(
+                src_ref=hsend.at[which, bands],
+                dst_ref=hrecv.at[n, bands],
+                send_sem=h_send.at[group, n],
+                recv_sem=h_recv.at[group, n],
+                device_id=around(dy, dx),
+                device_id_type=MESH,
+            )
+            copy.start()
+            halo.append(copy)
+
     for n in range(6 + 4):
         if n < 6:
-            todo.append((reduce_tiles, n))
+            reduce_tiles(ORDER[n])
         if 0 <= n - 2 < 6:
-            todo.append((second, n - 2))
+            second(ORDER[n - 2])
         if 0 <= n - 4 < 6:
-            todo.append((third, n - 4))
-    for step_fn, n in todo:
-        step_fn(ORDER[n])
-
-    halo = []
-    for n, (dy, dx) in enumerate(AROUND):
-        which = 0 if dy < 0 else 1 if dy > 0 else 2 if dx < 0 else 3
-        copy = pltpu.make_async_remote_copy(
-            src_ref=hsend.at[which],
-            dst_ref=hrecv.at[n],
-            send_sem=h_send.at[n],
-            recv_sem=h_recv.at[n],
-            device_id=around(dy, dx),
-            device_id_type=MESH,
-        )
-        copy.start()
-        halo.append(copy)
+            third(ORDER[n - 4])
+            if n - 4 in (2, 5):
+                send_halo((n - 4) // 3)
+
     for b in ORDER:
         for copy in s1[b][1:] + s2[b] + s3[b]:
             copy.wait_send()
     for n, copy in enumerate(halo):
         copy.wait_recv()
-        out_ref[768 + 48 * n : 816 + 48 * n, :] = hrecv[n].reshape(48, 128)
+        group, slot = n // 8, n % 8
+        for k in range(3):
+            r = 768 + 48 * slot + 8 * ORDER[3 * group + k]
+            out_ref[r : r + 8, :] = hrecv[slot, 3 * group + k]
     for copy in halo:
         copy.wait_send()
 
@@ -299,10 +327,16 @@
             pltpu.VMEM((3, 256, 4096), BF16),
             pltpu.VMEM((3, 256, 4224), BF16),
             pltpu.VMEM((3, 256, 4096), BF16),
-            pltpu.VMEM((NB, 128, WIDE), F32),
-            pltpu.VMEM((NB, 3, 32, WIDE), F32),
-            pltpu.VMEM((NB, 32, WIDE), F32),
-            pltpu.VMEM((NB, 3, 8, WIDE), F32),
+            pltpu.VMEM((NB, 128, HALF), F32),
+            pltpu.VMEM((NB, 128, QUARTER), jnp.int32),
+            pltpu.VMEM((NB, 128, 128), F32),
+            pltpu.VMEM((NB, 3, 32, QUARTER), jnp.int32),
+            pltpu.VMEM((NB, 3, 32, 128), F32),
+            pltpu.VMEM((NB, 32, HALF), F32),
+            pltpu.VMEM((NB, 32, QUARTER), jnp.int32),
+            pltpu.VMEM((NB, 32, 128), F32),
+            pltpu.VMEM((NB, 3, 8, QUARTER), jnp.int32),
+            pltpu.VMEM((NB, 3, 8, 128), F32),
             pltpu.VMEM((128, 128), F32),
             pltpu.VMEM((4, NB, 8, 128), F32),
             pltpu.VMEM((8, NB, 8, 128), F32),
@@ -310,12 +344,12 @@
             dma((NB,)),
             dma((NB, 7)),
             dma((NB, 7)),
-            dma((NB, 3)),
-            dma((NB, 3)),
-            dma((NB, 3)),
-            dma((NB, 3)),
-            dma((8,)),
-            dma((8,)),
+            dma((NB, 3, 2)),
+            dma((NB, 3, 2)),
+            dma((NB, 3, 2)),
+            dma((NB, 3, 2)),
+            dma((2, 8)),
+            dma((2, 8)),
         ],
         compiler_params=pltpu.CompilerParams(
             collective_id=0, has_side_effects=True, vmem_limit_bytes=60 * 1024 * 1024

time: 130 us -> 113 us (0.87)
  Pallas kernels: 128 us -> 111 us
    pallas_call x1, Pallas kernels: 110 us -> 92.4 us  [exchange(): pl.pallas_call(exchange_kernel, out_shape=jax.ShapeDtypeStruct((1248, 128...]
where the time goes in v3:
time: 113 us
  Pallas kernels  111 us (98%)
    pallas_call x1, Pallas kernels, exchange(): pl.pallas_call(exchange_kernel, out_shape=jax.ShapeDtypeStruct((1248, 128...  92.4 us
    pallas_call x1, Pallas kernels, detect(): pl.pallas_call(detect_kernel, out_shape=(jax.ShapeDtypeStruct((NB, 128, 1...  18.7 us

profile of v3, /device:TPU:1, one launch (start us, length us, event | category | flops | bytes accessed | tf_op | source)
XLA Modules:
  0.0 112.8 jit_solution(15801824440944008398)
XLA Ops:
  0.6 0.0 copy-start.5
  0.6 0.0 copy-start.1
  0.7 0.0 copy-start.4
  0.7 0.0 copy-start.3
  0.7 0.0 copy-start.2
  0.7 92.4 %tile_exchange.1.coadd_ref = f32[1248,128]{1,0:T(8,128)} custom-call(bf16[6,128,4096]{2,1,0:T(8,128)(2,1)} %bitcast.14, bf16[6,128]{1,0:T(8,128)(2,1)} %bitcast.15, s32[1,128]{1,0:T(1,128)} %bitcast.16, s32[1,128]{1,0:T(1,128)} %bitcast.17), custom_call_target="tpu_custom_call" | custom-call | tf_op jit(solution)/shard_map/tile_exchange/pallas_call | solution.py:316
  93.1 0.0 copy-done.5
  93.1 0.0 copy-done.1
  93.1 0.0 copy-done.4
  93.1 0.0 copy-done.3
  93.1 0.0 copy-done.2
  93.1 0.0 copy-start
  93.1 1.1 copy-done
  94.2 18.7 %detect.1 = (bf16[6,128,128]{2,1,0:T(8,128)(2,1)}, bf16[64,128,128]{2,1,0:T(8,128)(2,1)}) custom-call(f32[9,6,9]{2,1,0:T(8,128)S(1)} %bitcast.10, f32[1248,128]{1,0:T(8,128)S(1)} %copy-done, bf16[6,3,3,64]{3,2,1,0:T(4,128)(2,1)S(1)} %bitcast.11, f32[1,64]{1,0:T(1,128)S(1)} %bitcast.12, bf16[3,3,64,64]{3,2,1,0:T(8,128)(2,1)S(1)} %bitcast.9, f32[1,64]{1,0:T(1,128)S(1)} %bitcast.13), custom_call_target="tpu_custom_call" | custom-call | tf_op jit(solution)/shard_map/detect/pallas_call | solution.py:577
Async XLA Ops:
  0.6 92.4 %copy-start.5 = (f32[64]{0:T(128)S(1)}, f32[64]{0:T(128)}, u32[]{:S(2)}) copy-start(f32[64]{0:T(128)} %param.17) | copy-start | bytes 772
  0.6 92.4 %copy-start.1 = (bf16[64,64,3,3]{1,0,3,2:T(8,128)(2,1)S(1)}, bf16[64,64,3,3]{1,0,3,2:T(8,128)(2,1)}, u32[]{:S(2)}) copy-start(bf16[64,64,3,3]{1,0,3,2:T(8,128)(2,1)} %param.16) | copy-start | bytes 221188
  0.7 92.4 %copy-start.4 = (f32[64]{0:T(128)S(1)}, f32[64]{0:T(128)}, u32[]{:S(2)}) copy-start(f32[64]{0:T(128)} %param.15) | copy-start | bytes 772
  0.7 92.4 %copy-start.3 = (bf16[64,6,3,3]{0,3,2,1:T(4,128)(2,1)S(1)}, bf16[64,6,3,3]{0,3,2,1:T(4,128)(2,1)}, u32[]{:S(2)}) copy-start(bf16[64,6,3,3]{0,3,2,1:T(4,128)(2,1)} %param.14) | copy-start | bytes 20740
  0.7 92.4 %copy-start.2 = (f32[6,9,9]{2,0,1:T(8,128)S(1)}, f32[6,9,9]{2,0,1:T(8,128)}, u32[]{:S(2)}) copy-start(f32[6,9,9]{2,0,1:T(8,128)} %param.13) | copy-start | bytes 5836
  93.1 1.1 copy-start

commit v4 on v3

--- a/solution.py
+++ b/solution.py
@@ -14,12 +14,424 @@
 NB = 6
 HALF = 2048
 QUARTER = 1024
+WIDE = HALF + 128
 ORDER = (0, 2, 4, 1, 3, 5)
 MEMBERS = ((2, 0), (2, 1), (1, 0), (3, 0), (1, 1), (3, 1), (0, 1))
 AROUND = ((-1, 0), (1, 0), (0, -1), (0, 1), (-1, -1), (-1, 1), (1, -1), (1, 1))
 
 
+def encode(values, denom, flag, size):
+    top = jnp.max(jnp.abs(values), axis=1, keepdims=True)
+    some = top > 1e-30
+    inverse = jnp.where(some, 32767.0 / jnp.where(some, top, 1.0), 0.0)
+    codes = (values * inverse + 32768.5).astype(jnp.int32)
+    words = codes[:, :QUARTER] | (codes[:, QUARTER:] << 16)
+    lane = lax.broadcasted_iota(jnp.int32, (size, 128), 1)
+    extra = jnp.where(lane < 64, denom, top * (1.0 / 32767.0))
+    return words, jnp.where(lane == 127, flag, extra)
+
+
+def decode(words, extra):
+    step = extra[:, 64:65]
+    low = (words & 65535).astype(F32) - 32768.0
+    high = lax.shift_right_logical(words, jnp.full_like(words, 16)).astype(F32) - 32768.0
+    return low * step, high * step
+
+
+def gathered(own, own_extra, words, extras):
+    low, high = own[:, :QUARTER], own[:, QUARTER:]
+    denom, flag = own_extra[:, 0:1], own_extra[:, 127:128]
+    for k in range(3):
+        a, c = decode(words[k], extras[k])
+        low, high, denom = low + a, high + c, denom + extras[k][:, 0:1]
+        flag = jnp.maximum(flag, extras[k][:, 127:128])
+    return low, high, denom, jnp.max(flag, axis=0, keepdims=True)
+
+
 def exchange_kernel(
+    tiles_hbm,
+    wt_ref,
+    own_ref,
+    cell_ref,
+    out_ref,
+    tin,
+    sel,
+    selx,
+    meta,
+    send_lo,
+    send_hi,
+    send_x,
+    recv_lo,
+    recv_hi,
+    recv_x,
+    acc2,
+    st2,
+    st2m,
+    rcv2,
+    rcv2m,
+    acc3,
+    st3,
+    st3m,
+    rcv3,
+    rcv3m,
+    tbuf,
+    rbuf,
+    hsend,
+    hrecv,
+    tin_sem,
+    self_sem,
+    s1_send,
+    s1_recv,
+    x_send,
+    x_recv,
+    s2_send,
+    s2_recv,
+    s3_send,
+    s3_recv,
+    c_send,
+    c_recv,
+    h_send,
+    h_recv,
+):
+    ix = lax.axis_index("skyx")
+    iy = lax.axis_index("skyy")
+    core = ix % 2
+    q = (ix // 2, iy % 4, iy // 4)
+
+    def device(axis, step, flip):
+        r = list(q)
+        if step:
+            r[axis] = (r[axis] + step) % 4
+        c = (core + flip) % 2 if flip else core
+        return (r[0] * 2 + c, r[2] * 4 + r[1])
+
+    def around(dy, dx):
+        return ((ix + dx + 8) % 8, (iy + dy + 16) % 16)
+
+    barrier = pltpu.get_barrier_semaphore()
+    peers = [device(0, 0, 1)]
+    for axis in range(3):
+        for step, flip in MEMBERS[:6]:
+            peers.append(device(axis, step, flip))
+    for dy, dx in AROUND:
+        peers.append(around(dy, dx))
+    for peer in peers:
+        pl.semaphore_signal(barrier, inc=1, device_id=peer, device_id_type=MESH)
+
+    tin_copies = []
+    for b in range(NB):
+        tin_copies.append(pltpu.make_async_copy(tiles_hbm.at[b], tin.at[b], tin_sem.at[b]))
+        tin_copies[b].start()
+
+    own = own_ref[...]
+    ox, oy = own // 16, own % 16
+    oq = (ox // 2, oy % 4, oy // 4)
+    oc = ox % 2
+    earlier = lax.broadcasted_iota(jnp.int32, (128, 128), 0) < lax.broadcasted_iota(
+        jnp.int32, (128, 128), 1
+    )
+    rows = lax.broadcasted_iota(jnp.int32, (128, 128), 0)
+    rows_x = lax.broadcasted_iota(jnp.int32, (64, 128), 0)
+    lane128 = lax.broadcasted_iota(jnp.int32, (128, 128), 1)
+    most = jnp.zeros((1, 128), F32)
+    codes = []
+    for p in range(3):
+        group = jnp.broadcast_to(oq[p].astype(F32), (128, 128))
+        rank = jnp.sum(
+            jnp.where((group == group.T) & earlier, 1.0, 0.0), axis=0, keepdims=True
+        )
+        most = jnp.maximum(most, rank)
+        rank = rank.astype(jnp.int32)
+        slot = jnp.where(rank < 32, oq[p] * 32 + rank, -1)
+        sel[p] = jnp.where(rows == slot, 1.0, 0.0).astype(BF16)
+        slot = jnp.where((rank >= 32) & (rank < 40), oq[p] * 16 + rank - 32, -64)
+        selx[p, 0] = jnp.where(rows_x == slot, 1.0, 0.0).astype(BF16)
+        selx[p, 1] = jnp.where(rows_x == slot + 8, 1.0, 0.0).astype(BF16)
+        unit = oq[(p + 1) % 3] * 4 + oq[(p + 2) % 3]
+        codes.append(((unit * 2 + oc) * 4 + cell_ref[...] + 1).astype(F32))
+    over = jnp.where(jnp.max(most, axis=1, keepdims=True) > 39.5, 1.0, 0.0)
+    meta[...] = jnp.zeros((128, 128), F32)
+    meta[0:6, :] = wt_ref[...].astype(F32)
+
+    def pick(which, value):
+        return jnp.dot(which, value, preferred_element_type=F32)
+
+    def pick_meta(which):
+        return lax.dot_general(
+            which,
+            meta[...].astype(BF16),
+            (((1,), (1,)), ((), ())),
+            preferred_element_type=F32,
+        )
+
+    s1 = {}
+    for n in range(NB):
+        p, half = n % 3, n // 3
+        if half == 0:
+            tin_copies[2 * p].wait()
+            tin_copies[2 * p + 1].wait()
+            meta[6:7, :] = codes[p]
+            flagged = jnp.where(lane128 == 7, over, pick_meta(sel[p])).astype(BF16)
+            extra = (pick_meta(selx[p, 0]) + pick_meta(selx[p, 1])).astype(BF16)
+        for k in range(2):
+            b = 2 * p + k
+
+            def gather(c, carry, b=b, p=p, k=k, half=half):
+                at = pl.ds(pl.multiple_of(c * 512, 512), 512)
+                there = pl.ds(pl.multiple_of(c * 512 + HALF, 512), 512)
+                if half == 0:
+                    send_lo[p, k, :, at] = pick(sel[p], tin[b, :, at]).astype(BF16)
+                    send_x[p, k, :, at] = (
+                        pick(selx[p, 0], tin[b, :, at]) + pick(selx[p, 1], tin[b, :, there])
+                    ).astype(BF16)
+                else:
+                    send_hi[p, k, :, at] = pick(sel[p], tin[b, :, there]).astype(BF16)
+                return carry
+
+            lax.fori_loop(0, 4, gather, 0)
+            if half == 0:
+                send_lo[p, k, :, HALF:WIDE] = flagged
+                send_x[p, k, :, HALF:WIDE] = extra
+        if n == 0:
+            pl.semaphore_wait(barrier, len(peers))
+        mine = q[p] * 2 + core
+        streams = [(send_hi, recv_hi, 32, s1_send, s1_recv)]
+        if half == 0:
+            streams = [
+                (send_lo, recv_lo, 32, s1_send, s1_recv),
+                (send_x, recv_x, 16, x_send, x_recv),
+            ]
+        local, away = [], []
+        for m, (step, flip) in enumerate(MEMBERS + ((0, 0),)):
+            to = (q[p] + step) % 4
+            parity = (core + flip) % 2
+            for w, (src, dst, size, sends, recvs) in enumerate(streams):
+                from_ref = src.at[p, parity, pl.ds(pl.multiple_of(to * size, size), size)]
+                to_ref = dst.at[p, pl.ds(pl.multiple_of(mine * size, size), size)]
+                if (step, flip) == (0, 0):
+                    copy = pltpu.make_async_copy(from_ref, to_ref, self_sem.at[n, w])
+                    local.append(copy)
+                else:
+                    at = n if size == 32 else p
+                    copy = pltpu.make_async_remote_copy(
+                        src_ref=from_ref,
+                        dst_ref=to_ref,
+                        send_sem=sends.at[at, m],
+                        recv_sem=recvs.at[at, m],
+                        device_id=device(p, step, flip),
+                        device_id_type=MESH,
+                    )
+                    away.append(copy)
+                copy.start()
+        s1[n] = (local, away)
+
+    s2, s3, s4 = {}, {}, {}
+
+    def pass_on(n, axis, size, words, extras, to_words, to_extras, send, recv):
+        copies = []
+        for step in (2, 1, 3):
+            there = (q[axis] + step) % 4
+            at = pl.ds(pl.multiple_of(there * size, size), size)
+            for w, (src, dst) in enumerate(((words, to_words), (extras, to_extras))):
+                copy = pltpu.make_async_remote_copy(
+                    src_ref=src.at[n, at],
+                    dst_ref=dst.at[n, step - 1],
+                    send_sem=send.at[n, step - 1, w],
+                    recv_sem=recv.at[n, step - 1, w],
+                    device_id=device(axis, step, 0),
+                    device_id_type=MESH,
+                )
+                copy.start()
+                copies.append(copy)
+        return copies
+
+    weighted = {}
+
+    def coefficients(p):
+        m = recv_lo[p, :, HALF:WIDE].astype(F32).T
+        mx = recv_x[p, :, HALF:WIDE].astype(F32).T
+        w = jnp.where(core == 0, m[2 * p : 2 * p + 1], m[2 * p + 1 : 2 * p + 2])
+        wx = jnp.where(core == 0, mx[2 * p : 2 * p + 1], mx[2 * p + 1 : 2 * p + 2])
+        at = lax.broadcasted_iota(jnp.int32, (128, 256), 0).astype(F32) + 1.0
+        c = jnp.where(m[6:7] == at, jnp.broadcast_to(w, (128, 256)), 0.0)
+        cx = jnp.where(mx[6:7] == at[:, 0:128], jnp.broadcast_to(wx, (128, 128)), 0.0)
+        low = (lane128 // 8) % 2 == 0
+        x0, x1 = jnp.where(low, cx, 0.0), jnp.where(low, 0.0, cx)
+        denom = jnp.sum(c, axis=1, keepdims=True) + jnp.sum(x0, axis=1, keepdims=True)
+        flag = jnp.max(m[7:8], axis=1, keepdims=True)
+        return c.astype(BF16), x0.astype(BF16), x1.astype(BF16), denom, flag
+
+    def reduce_tiles(n):
+        p, half = n % 3, n // 3
+        for copy in s1[n][0]:
+            copy.wait()
+        for copy in s1[n][1]:
+            copy.wait_recv()
+        if half == 0:
+            weighted[p] = coefficients(p)
+        c, x0, x1, denom, flag = weighted[p]
+        src = recv_lo if half == 0 else recv_hi
+        cx = x0 if half == 0 else x1
+
+        def reduce(i, carry):
+            at = pl.ds(pl.multiple_of(i * 512, 512), 512)
+            acc2[n, :, at] = pick(c, src[p, :, at]) + pick(cx, recv_x[p, :, at])
+            return carry
+
+        lax.fori_loop(0, 4, reduce, 0)
+        st2[n], st2m[n] = encode(acc2[n], denom, flag, 128)
+        s2[n] = pass_on(n, (p + 1) % 3, 32, st2, st2m, rcv2, rcv2m, s2_send, s2_recv)
+
+    def second(n):
+        p = n % 3
+        for copy in s2[n]:
+            copy.wait_recv()
+        at = pl.ds(pl.multiple_of(q[(p + 1) % 3] * 32, 32), 32)
+        low, high, denom, flag = gathered(acc2[n, at, :], st2m[n, at, :], rcv2[n], rcv2m[n])
+        acc3[n, :, :QUARTER] = low
+        acc3[n, :, QUARTER:] = high
+        st3[n], st3m[n] = encode(acc3[n], denom, flag, 32)
+        s3[n] = pass_on(n, (p + 2) % 3, 8, st3, st3m, rcv3, rcv3m, s3_send, s3_recv)
+
+    def third(n):
+        p = n % 3
+        for copy in s3[n]:
+            copy.wait_recv()
+        at = pl.ds(pl.multiple_of(q[(p + 2) % 3] * 8, 8), 8)
+        low, high, denom, flag = gathered(acc3[n, at, :], st3m[n, at, :], rcv3[n], rcv3m[n])
+        if n == 0:
+            out_ref[1248:1256, :] = jnp.broadcast_to(flag, (8, 128))
+        scale = 1.0 / (1.0 + denom)
+        for j in range(8):
+            c = slice(128 * j, 128 * j + 128)
+            tbuf[n, pl.ds(j, 8, stride=16), :] = low[:, c] * scale
+            tbuf[n, pl.ds(j + 8, 8, stride=16), :] = high[:, c] * scale
+        s4[n] = pltpu.make_async_remote_copy(
+            src_ref=tbuf.at[n, pl.ds(pl.multiple_of((1 - core) * 64, 64), 64)],
+            dst_ref=rbuf.at[n],
+            send_sem=c_send.at[n],
+            recv_sem=c_recv.at[n],
+            device_id=device(0, 0, 1),
+            device_id_type=MESH,
+        )
+        s4[n].start()
+
+    left_half = lax.broadcasted_iota(jnp.int32, (16, 128), 1) < 64
+    halo = []
+
+    def place(value, band, half):
+        for cy in range(2):
+            a, c = value[32 * cy : 32 * cy + 16], value[32 * cy + 16 : 32 * cy + 32]
+            y0 = band * 128 + 64 * cy + 32 * half
+            out_ref[pl.ds(y0, 16, stride=2), :] = jnp.where(left_half, a, pltpu.roll(c, 64, 1))
+            out_ref[pl.ds(y0 + 1, 16, stride=2), :] = jnp.where(
+                left_half, pltpu.roll(a, 64, 1), c
+            )
+
+    def fourth(n):
+        p, half = n % 3, n // 3
+        place(tbuf[n, pl.ds(pl.multiple_of(core * 64, 64), 64), :], 2 * p + core, half)
+        s4[n].wait_recv()
+        place(rbuf[n], 2 * p + 1 - core, half)
+        if half == 0:
+            return
+        for b in (2 * p, 2 * p + 1):
+            r = 128 * b
+            hsend[0, b] = out_ref[r : r + 8, :]
+            hsend[1, b] = out_ref[r + 120 : r + 128, :]
+            turned = out_ref[r : r + 128, :].T
+            hsend[2, b] = turned[0:8, :]
+            hsend[3, b] = turned[120:128, :]
+            out_ref[1152 + 8 * b : 1160 + 8 * b, :] = turned[0:8, :]
+            out_ref[1200 + 8 * b : 1208 + 8 * b, :] = turned[120:128, :]
+        bands = pl.ds(2 * p, 2)
+        for m, (dy, dx) in enumerate(AROUND):
+            which = 0 if dy < 0 else 1 if dy > 0 else 2 if dx < 0 else 3
+            copy = pltpu.make_async_remote_copy(
+                src_ref=hsend.at[which, bands],
+                dst_ref=hrecv.at[m, bands],
+                send_sem=h_send.at[p, m],
+                recv_sem=h_recv.at[p, m],
+                device_id=around(dy, dx),
+                device_id_type=MESH,
+            )
+            copy.start()
+            halo.append(copy)
+
+    steps = (reduce_tiles, second, third, fourth)
+    for n in range(6 + 6):
+        for lag, step in zip((0, 2, 4, 5), steps):
+            if 0 <= n - lag < 6:
+                step(n - lag)
+
+    for n in range(NB):
+        for copy in s1[n][1] + s2[n] + s3[n] + [s4[n]]:
+            copy.wait_send()
+    for n, copy in enumerate(halo):
+        copy.wait_recv()
+        p, slot = n // 8, n % 8
+        r = 768 + 48 * slot + 16 * p
+        out_ref[r : r + 16, :] = hrecv[slot, 2 * p : 2 * p + 2].reshape(16, 128)
+    for copy in halo:
+        copy.wait_send()
+
+
+def exchange(tiles, weights, owners, cells):
+    vmem = pl.BlockSpec(memory_space=pltpu.VMEM)
+    dma = pltpu.SemaphoreType.DMA
+    return pl.pallas_call(
+        exchange_kernel,
+        out_shape=jax.ShapeDtypeStruct((1256, 128), F32),
+        in_specs=[pl.BlockSpec(memory_space=pl.ANY), vmem, vmem, vmem],
+        out_specs=vmem,
+        scratch_shapes=[
+            pltpu.VMEM((NB, 128, 4096), BF16),
+            pltpu.VMEM((3, 128, 128), BF16),
+            pltpu.VMEM((3, 2, 64, 128), BF16),
+            pltpu.VMEM((128, 128), F32),
+            pltpu.VMEM((3, 2, 128, WIDE), BF16),
+            pltpu.VMEM((3, 2, 128, HALF), BF16),
+            pltpu.VMEM((3, 2, 64, WIDE), BF16),
+            pltpu.VMEM((3, 256, WIDE), BF16),
+            pltpu.VMEM((3, 256, HALF), BF16),
+            pltpu.VMEM((3, 128, WIDE), BF16),
+            pltpu.VMEM((NB, 128, HALF), F32),
+            pltpu.VMEM((NB, 128, QUARTER), jnp.int32),
+            pltpu.VMEM((NB, 128, 128), F32),
+            pltpu.VMEM((NB, 3, 32, QUARTER), jnp.int32),
+            pltpu.VMEM((NB, 3, 32, 128), F32),
+            pltpu.VMEM((NB, 32, HALF), F32),
+            pltpu.VMEM((NB, 32, QUARTER), jnp.int32),
+            pltpu.VMEM((NB, 32, 128), F32),
+            pltpu.VMEM((NB, 3, 8, QUARTER), jnp.int32),
+            pltpu.VMEM((NB, 3, 8, 128), F32),
+            pltpu.VMEM((NB, 128, 128), F32),
+            pltpu.VMEM((NB, 64, 128), F32),
+            pltpu.VMEM((4, NB, 8, 128), F32),
+            pltpu.VMEM((8, NB, 8, 128), F32),
+            dma((NB,)),
+            dma((NB, 2)),
+            dma((NB, 7)),
+            dma((NB, 7)),
+            dma((3, 7)),
+            dma((3, 7)),
+            dma((NB, 3, 2)),
+            dma((NB, 3, 2)),
+            dma((NB, 3, 2)),
+            dma((NB, 3, 2)),
+            dma((NB,)),
+            dma((NB,)),
+            dma((3, 8)),
+            dma((3, 8)),
+        ],
+        compiler_params=pltpu.CompilerParams(
+            collective_id=0, has_side_effects=True, vmem_limit_bytes=60 * 1024 * 1024
+        ),
+        name="tile_exchange",
+    )(tiles, weights, owners, cells)
+
+
+def full_exchange_kernel(
     tiles_hbm,
     wt_ref,
     own_ref,
@@ -306,16 +718,17 @@
         for k in range(3):
             r = 768 + 48 * slot + 8 * ORDER[3 * group + k]
             out_ref[r : r + 8, :] = hrecv[slot, 3 * group + k]
+    out_ref[1248:1256, :] = jnp.zeros((8, 128), F32)
     for copy in halo:
         copy.wait_send()
 
 
-def exchange(tiles, weights, owners, cells):
+def full_exchange(tiles, weights, owners, cells):
     vmem = pl.BlockSpec(memory_space=pltpu.VMEM)
     dma = pltpu.SemaphoreType.DMA
     return pl.pallas_call(
-        exchange_kernel,
-        out_shape=jax.ShapeDtypeStruct((1248, 128), F32),
+        full_exchange_kernel,
+        out_shape=jax.ShapeDtypeStruct((1256, 128), F32),
         in_specs=[pl.BlockSpec(memory_space=pl.ANY), vmem, vmem, vmem],
         out_specs=vmem,
         scratch_shapes=[
@@ -352,9 +765,9 @@
             dma((2, 8)),
         ],
         compiler_params=pltpu.CompilerParams(
-            collective_id=0, has_side_effects=True, vmem_limit_bytes=60 * 1024 * 1024
+            collective_id=1, has_side_effects=True, vmem_limit_bytes=60 * 1024 * 1024
         ),
-        name="tile_exchange",
+        name="full_exchange",
     )(tiles, weights, owners, cells)
 
 
@@ -611,12 +1024,14 @@
     conv2_weight,
     conv2_bias,
 ):
-    coadd = exchange(
+    operands = (
         tiles.transpose(1, 0, 2),
         tile_weight.transpose(1, 0),
         owners.reshape(1, 128),
         cells.reshape(1, 128),
     )
+    coadd = exchange(*operands)
+    coadd = lax.cond(coadd[1248, 0] > 0.5, lambda: full_exchange(*operands), lambda: coadd)
     return detect(
         psf_kernel.transpose(1, 0, 2),
         coadd,

time: 113 us -> 97.3 us (0.86)
  Pallas kernels: 111 us -> 95 us
    pallas_call x1, Pallas kernels: 92.4 us -> 76.3 us  [exchange(): pl.pallas_call(exchange_kernel, out_shape=jax.ShapeDtypeStruct((1256, 128...]
where the time goes in v4:
time: 97.3 us; the launch traced here: 97.2 us
  Pallas kernels  95 us (98%)
  between operations  1.43 us (1%)
    pallas_call x1, Pallas kernels, exchange(): pl.pallas_call(exchange_kernel, out_shape=jax.ShapeDtypeStruct((1256, 128...  76.3 us
    pallas_call x1, Pallas kernels, detect(): pl.pallas_call(detect_kernel, out_shape=(jax.ShapeDtypeStruct((NB, 128, 1...  18.7 us

profile of v4, /device:TPU:1, one launch (start us, length us, event | category | flops | bytes accessed | tf_op | source)
XLA Modules:
  0.0 97.2 jit_solution(10507204150857385117)
XLA Ops:
  0.6 0.0 copy-start.7
  0.6 0.0 copy-start.6
  0.7 0.0 copy-start.5
  0.7 0.0 copy-start
  0.7 0.0 copy-start.1
  0.7 0.0 copy-start.2
  0.7 0.0 copy-start.3
  0.7 0.0 copy-start.4
  0.7 76.3 %tile_exchange.1 = f32[1256,128]{1,0:T(8,128)S(1)} custom-call(bf16[6,128,4096]{2,1,0:T(8,128)(2,1)} %bitcast.15, bf16[6,128]{1,0:T(8,128)(2,1)} %bitcast.17, s32[1,128]{1,0:T(1,128)} %bitcast.19, s32[1,128]{1,0:T(1,128)} %bitcast.21), custom_call_target="tpu_custom_call" | custom-call | tf_op jit(solution)/shard_map/tile_exchange/pallas_call | solution.py:382
  77.1 0.5 slice.3
  78.2 0.0 copy-done.7
  78.2 0.0 copy-done.6
  78.3 0.0 copy-done.5
  78.3 0.2 conditional.1
  78.5 0.0 copy-done
  78.5 0.0 copy-done.1
  78.5 0.0 copy-done.2
  78.5 0.0 copy-done.3
  78.5 0.0 copy-done.4
  78.5 18.7 %detect.1 = (bf16[6,128,128]{2,1,0:T(8,128)(2,1)}, bf16[64,128,128]{2,1,0:T(8,128)(2,1)}) custom-call(f32[9,6,9]{2,1,0:T(8,128)S(1)} %bitcast.11, f32[1256,128]{1,0:T(8,128)S(1)} %get-tuple-element.18.coadd_ref, bf16[6,3,3,64]{3,2,1,0:T(4,128)(2,1)S(1)} %bitcast.12, f32[1,64]{1,0:T(1,128)S(1)} %bitcast.13, bf16[3,3,64,64]{3,2,1,0:T(8,128)(2,1)S(1)} %bitcast.10, ...), custom_call_target="tpu_custom_call" | custom-call | tf_op jit(solution)/shard_map/detect/pallas_call | solution.py:990
Async XLA Ops:
  0.6 77.6 %copy-start.7 = (s32[128]{0:T(128)S(1)}, s32[128]{0:T(128)}, u32[]{:S(2)}) copy-start(s32[128]{0:T(128)} %param.14) | copy-start | bytes 1540
  0.6 77.6 %copy-start.6 = (s32[128,1]{0,1:T(1,128)S(1)}, s32[128,1]{0,1:T(1,128)}, u32[]{:S(2)}) copy-start(s32[128,1]{0,1:T(1,128)} %param.13) | copy-start | bytes 1540
  0.7 77.6 %copy-start.5 = (bf16[128,6]{0,1:T(8,128)(2,1)S(1)}, bf16[128,6]{0,1:T(8,128)(2,1)}, u32[]{:S(2)}) copy-start(bf16[128,6]{0,1:T(8,128)(2,1)} %param.12) | copy-start | bytes 4612
  0.7 77.8 %copy-start = (bf16[64,64,3,3]{1,0,3,2:T(8,128)(2,1)S(1)}, bf16[64,64,3,3]{1,0,3,2:T(8,128)(2,1)}, u32[]{:S(2)}) copy-start(bf16[64,64,3,3]{1,0,3,2:T(8,128)(2,1)} %param.18) | copy-start | bytes 221188
  0.7 77.8 %copy-start.1 = (f32[6,9,9]{2,0,1:T(8,128)S(1)}, f32[6,9,9]{2,0,1:T(8,128)}, u32[]{:S(2)}) copy-start(f32[6,9,9]{2,0,1:T(8,128)} %param.15) | copy-start | bytes 5836
  0.7 77.8 %copy-start.2 = (bf16[64,6,3,3]{0,3,2,1:T(4,128)(2,1)S(1)}, bf16[64,6,3,3]{0,3,2,1:T(4,128)(2,1)}, u32[]{:S(2)}) copy-start(bf16[64,6,3,3]{0,3,2,1:T(4,128)(2,1)} %param.16) | copy-start | bytes 20740
  0.7 77.8 %copy-start.3 = (f32[64]{0:T(128)S(1)}, f32[64]{0:T(128)}, u32[]{:S(2)}) copy-start(f32[64]{0:T(128)} %param.17) | copy-start | bytes 772
  0.7 77.8 %copy-start.4 = (f32[64]{0:T(128)S(1)}, f32[64]{0:T(128)}, u32[]{:S(2)}) copy-start(f32[64]{0:T(128)} %param.19) | copy-start | bytes 772

commit v5 on v4

--- a/solution.py
+++ b/solution.py
@@ -15,6 +15,9 @@
 HALF = 2048
 QUARTER = 1024
 WIDE = HALF + 128
+PIECES = ((0, 0, 2048), (1, 0, 2048))
+UNITS = 3 * len(PIECES)
+LAGS = (0, 2, 4, 5)
 ORDER = (0, 2, 4, 1, 3, 5)
 MEMBERS = ((2, 0), (2, 1), (1, 0), (3, 0), (1, 1), (3, 1), (0, 1))
 AROUND = ((-1, 0), (1, 0), (0, -1), (0, 1), (-1, -1), (-1, 1), (1, -1), (1, 1))
@@ -25,7 +28,8 @@
     some = top > 1e-30
     inverse = jnp.where(some, 32767.0 / jnp.where(some, top, 1.0), 0.0)
     codes = (values * inverse + 32768.5).astype(jnp.int32)
-    words = codes[:, :QUARTER] | (codes[:, QUARTER:] << 16)
+    middle = values.shape[1] // 2
+    words = codes[:, :middle] | (codes[:, middle:] << 16)
     lane = lax.broadcasted_iota(jnp.int32, (size, 128), 1)
     extra = jnp.where(lane < 64, denom, top * (1.0 / 32767.0))
     return words, jnp.where(lane == 127, flag, extra)
@@ -39,7 +43,8 @@
 
 
 def gathered(own, own_extra, words, extras):
-    low, high = own[:, :QUARTER], own[:, QUARTER:]
+    middle = own.shape[1] // 2
+    low, high = own[:, :middle], own[:, middle:]
     denom, flag = own_extra[:, 0:1], own_extra[:, 127:128]
     for k in range(3):
         a, c = decode(words[k], extras[k])
@@ -133,25 +138,26 @@
     rows = lax.broadcasted_iota(jnp.int32, (128, 128), 0)
     rows_x = lax.broadcasted_iota(jnp.int32, (64, 128), 0)
     lane128 = lax.broadcasted_iota(jnp.int32, (128, 128), 1)
-    most = jnp.zeros((1, 128), F32)
-    codes = []
-    for p in range(3):
+    meta[...] = jnp.zeros((128, 128), F32)
+    meta[0:6, :] = wt_ref[...].astype(F32)
+
+    def select(p):
         group = jnp.broadcast_to(oq[p].astype(F32), (128, 128))
         rank = jnp.sum(
             jnp.where((group == group.T) & earlier, 1.0, 0.0), axis=0, keepdims=True
         )
-        most = jnp.maximum(most, rank)
+        over = jnp.where(jnp.max(rank, axis=1, keepdims=True) > 39.5, 1.0, 0.0)
         rank = rank.astype(jnp.int32)
         slot = jnp.where(rank < 32, oq[p] * 32 + rank, -1)
-        sel[p] = jnp.where(rows == slot, 1.0, 0.0).astype(BF16)
+        sel[p, 0:128] = jnp.where(rows == slot, 1.0, 0.0).astype(BF16)
         slot = jnp.where((rank >= 32) & (rank < 40), oq[p] * 16 + rank - 32, -64)
-        selx[p, 0] = jnp.where(rows_x == slot, 1.0, 0.0).astype(BF16)
-        selx[p, 1] = jnp.where(rows_x == slot + 8, 1.0, 0.0).astype(BF16)
+        sel[p, 128:192] = jnp.where(rows_x == slot, 1.0, 0.0).astype(BF16)
+        selx[p] = jnp.where(rows_x == slot + 8, 1.0, 0.0).astype(BF16)
         unit = oq[(p + 1) % 3] * 4 + oq[(p + 2) % 3]
-        codes.append(((unit * 2 + oc) * 4 + cell_ref[...] + 1).astype(F32))
-    over = jnp.where(jnp.max(most, axis=1, keepdims=True) > 39.5, 1.0, 0.0)
-    meta[...] = jnp.zeros((128, 128), F32)
-    meta[0:6, :] = wt_ref[...].astype(F32)
+        meta[6:7, :] = ((unit * 2 + oc) * 4 + cell_ref[...] + 1).astype(F32)
+        both = pick_meta(sel[p])
+        extra = both[128:192] + pick_meta(selx[p])
+        return jnp.where(lane128 == 7, over, both[0:128]).astype(BF16), extra.astype(BF16)
 
     def pick(which, value):
         return jnp.dot(which, value, preferred_element_type=F32)
@@ -165,49 +171,48 @@
         )
 
     s1 = {}
-    for n in range(NB):
-        p, half = n % 3, n // 3
+    for n in range(UNITS):
+        p, (half, first, width) = n % 3, PIECES[n // 3]
         if half == 0:
-            tin_copies[2 * p].wait()
-            tin_copies[2 * p + 1].wait()
-            meta[6:7, :] = codes[p]
-            flagged = jnp.where(lane128 == 7, over, pick_meta(sel[p])).astype(BF16)
-            extra = (pick_meta(selx[p, 0]) + pick_meta(selx[p, 1])).astype(BF16)
+            flagged, extra = select(p)
         for k in range(2):
             b = 2 * p + k
-
-            def gather(c, carry, b=b, p=p, k=k, half=half):
-                at = pl.ds(pl.multiple_of(c * 512, 512), 512)
-                there = pl.ds(pl.multiple_of(c * 512 + HALF, 512), 512)
+            if half == 0:
+                tin_copies[b].wait()
+
+            def gather(c, carry, b=b, p=p, k=k, half=half, first=first):
+                at = pl.ds(pl.multiple_of(c * 512 + first, 512), 512)
+                there = pl.ds(pl.multiple_of(c * 512 + first + HALF, 512), 512)
                 if half == 0:
-                    send_lo[p, k, :, at] = pick(sel[p], tin[b, :, at]).astype(BF16)
+                    both = pick(sel[p], tin[b, :, at])
+                    send_lo[p, k, :, at] = both[0:128].astype(BF16)
                     send_x[p, k, :, at] = (
-                        pick(selx[p, 0], tin[b, :, at]) + pick(selx[p, 1], tin[b, :, there])
+                        both[128:192] + pick(selx[p], tin[b, :, there])
                     ).astype(BF16)
                 else:
-                    send_hi[p, k, :, at] = pick(sel[p], tin[b, :, there]).astype(BF16)
+                    send_hi[p, k, :, at] = pick(sel[p, 0:128], tin[b, :, there]).astype(BF16)
                 return carry
 
-            lax.fori_loop(0, 4, gather, 0)
+            lax.fori_loop(0, width // 512, gather, 0)
             if half == 0:
                 send_lo[p, k, :, HALF:WIDE] = flagged
                 send_x[p, k, :, HALF:WIDE] = extra
         if n == 0:
             pl.semaphore_wait(barrier, len(peers))
         mine = q[p] * 2 + core
-        streams = [(send_hi, recv_hi, 32, s1_send, s1_recv)]
+        streams = [(send_hi, recv_hi, 32, pl.ds(first, width), s1_send, s1_recv)]
         if half == 0:
             streams = [
-                (send_lo, recv_lo, 32, s1_send, s1_recv),
-                (send_x, recv_x, 16, x_send, x_recv),
+                (send_lo, recv_lo, 32, pl.ds(0, WIDE), s1_send, s1_recv),
+                (send_x, recv_x, 16, pl.ds(0, WIDE), x_send, x_recv),
             ]
         local, away = [], []
         for m, (step, flip) in enumerate(MEMBERS + ((0, 0),)):
             to = (q[p] + step) % 4
             parity = (core + flip) % 2
-            for w, (src, dst, size, sends, recvs) in enumerate(streams):
-                from_ref = src.at[p, parity, pl.ds(pl.multiple_of(to * size, size), size)]
-                to_ref = dst.at[p, pl.ds(pl.multiple_of(mine * size, size), size)]
+            for w, (src, dst, size, columns, sends, recvs) in enumerate(streams):
+                from_ref = src.at[p, parity, pl.ds(pl.multiple_of(to * size, size), size), columns]
+                to_ref = dst.at[p, pl.ds(pl.multiple_of(mine * size, size), size), columns]
                 if (step, flip) == (0, 0):
                     copy = pltpu.make_async_copy(from_ref, to_ref, self_sem.at[n, w])
                     local.append(copy)
@@ -229,13 +234,19 @@
 
     def pass_on(n, axis, size, words, extras, to_words, to_extras, send, recv):
         copies = []
+        half, first, width = PIECES[n // 3]
+        m, columns = 3 * half + n % 3, pl.ds(first // 2, width // 2)
         for step in (2, 1, 3):
             there = (q[axis] + step) % 4
             at = pl.ds(pl.multiple_of(there * size, size), size)
-            for w, (src, dst) in enumerate(((words, to_words), (extras, to_extras))):
+            pairs = (
+                (words.at[m, at, columns], to_words.at[m, step - 1, :, columns]),
+                (extras.at[n, at], to_extras.at[n, step - 1]),
+            )
+            for w, (from_ref, to_ref) in enumerate(pairs):
                 copy = pltpu.make_async_remote_copy(
-                    src_ref=src.at[n, at],
-                    dst_ref=dst.at[n, step - 1],
+                    src_ref=from_ref,
+                    dst_ref=to_ref,
                     send_sem=send.at[n, step - 1, w],
                     recv_sem=recv.at[n, step - 1, w],
                     device_id=device(axis, step, 0),
@@ -262,7 +273,8 @@
         return c.astype(BF16), x0.astype(BF16), x1.astype(BF16), denom, flag
 
     def reduce_tiles(n):
-        p, half = n % 3, n // 3
+        p, (half, first, width) = n % 3, PIECES[n // 3]
+        m = 3 * half + p
         for copy in s1[n][0]:
             copy.wait()
         for copy in s1[n][1]:
@@ -274,41 +286,59 @@
         cx = x0 if half == 0 else x1
 
         def reduce(i, carry):
-            at = pl.ds(pl.multiple_of(i * 512, 512), 512)
-            acc2[n, :, at] = pick(c, src[p, :, at]) + pick(cx, recv_x[p, :, at])
+            at = pl.ds(pl.multiple_of(i * 512 + first, 512), 512)
+            acc2[m, :, at] = pick(c, src[p, :, at]) + pick(cx, recv_x[p, :, at])
             return carry
 
-        lax.fori_loop(0, 4, reduce, 0)
-        st2[n], st2m[n] = encode(acc2[n], denom, flag, 128)
+        lax.fori_loop(0, width // 512, reduce, 0)
+        words, extra = encode(acc2[m, :, first : first + width], denom, flag, 128)
+        st2[m, :, first // 2 : (first + width) // 2] = words
+        st2m[n] = extra
         s2[n] = pass_on(n, (p + 1) % 3, 32, st2, st2m, rcv2, rcv2m, s2_send, s2_recv)
 
     def second(n):
-        p = n % 3
+        p, (half, first, width) = n % 3, PIECES[n // 3]
+        m, columns = 3 * half + p, slice(first // 2, (first + width) // 2)
         for copy in s2[n]:
             copy.wait_recv()
         at = pl.ds(pl.multiple_of(q[(p + 1) % 3] * 32, 32), 32)
-        low, high, denom, flag = gathered(acc2[n, at, :], st2m[n, at, :], rcv2[n], rcv2m[n])
-        acc3[n, :, :QUARTER] = low
-        acc3[n, :, QUARTER:] = high
-        st3[n], st3m[n] = encode(acc3[n], denom, flag, 32)
+        low, high, denom, flag = gathered(
+            acc2[m, at, first : first + width],
+            st2m[n, at, :],
+            rcv2[m, :, :, columns],
+            rcv2m[n],
+        )
+        middle = first + width // 2
+        acc3[m, :, first:middle] = low
+        acc3[m, :, middle : first + width] = high
+        st3[m, :, columns], st3m[n] = encode(acc3[m, :, first : first + width], denom, flag, 32)
         s3[n] = pass_on(n, (p + 2) % 3, 8, st3, st3m, rcv3, rcv3m, s3_send, s3_recv)
 
     def third(n):
-        p = n % 3
+        p, (half, first, width) = n % 3, PIECES[n // 3]
+        m, columns = 3 * half + p, slice(first // 2, (first + width) // 2)
         for copy in s3[n]:
             copy.wait_recv()
         at = pl.ds(pl.multiple_of(q[(p + 2) % 3] * 8, 8), 8)
-        low, high, denom, flag = gathered(acc3[n, at, :], st3m[n, at, :], rcv3[n], rcv3m[n])
-        if n == 0:
-            out_ref[1248:1256, :] = jnp.broadcast_to(flag, (8, 128))
+        low, high, denom, flag = gathered(
+            acc3[m, at, first : first + width],
+            st3m[n, at, :],
+            rcv3[m, :, :, columns],
+            rcv3m[n],
+        )
+        if n < 3:
+            flag = jnp.broadcast_to(flag, (8, 128))
+            out_ref[1248:1256, :] = jnp.maximum(out_ref[1248:1256, :], flag) if n else flag
         scale = 1.0 / (1.0 + denom)
-        for j in range(8):
+        lines = width // 128
+        for j in range(lines // 2):
             c = slice(128 * j, 128 * j + 128)
-            tbuf[n, pl.ds(j, 8, stride=16), :] = low[:, c] * scale
-            tbuf[n, pl.ds(j + 8, 8, stride=16), :] = high[:, c] * scale
+            tbuf[n, pl.ds(j, 8, stride=lines), :] = low[:, c] * scale
+            tbuf[n, pl.ds(j + lines // 2, 8, stride=lines), :] = high[:, c] * scale
+        size = 4 * lines
         s4[n] = pltpu.make_async_remote_copy(
-            src_ref=tbuf.at[n, pl.ds(pl.multiple_of((1 - core) * 64, 64), 64)],
-            dst_ref=rbuf.at[n],
+            src_ref=tbuf.at[n, pl.ds(pl.multiple_of((1 - core) * size, size), size)],
+            dst_ref=rbuf.at[n, pl.ds(0, size)],
             send_sem=c_send.at[n],
             recv_sem=c_recv.at[n],
             device_id=device(0, 0, 1),
@@ -316,24 +346,29 @@
         )
         s4[n].start()
 
-    left_half = lax.broadcasted_iota(jnp.int32, (16, 128), 1) < 64
     halo = []
 
-    def place(value, band, half):
+    def place(value, band, row):
+        lines = value.shape[0] // 4
+        left_half = lax.broadcasted_iota(jnp.int32, (lines, 128), 1) < 64
         for cy in range(2):
-            a, c = value[32 * cy : 32 * cy + 16], value[32 * cy + 16 : 32 * cy + 32]
-            y0 = band * 128 + 64 * cy + 32 * half
-            out_ref[pl.ds(y0, 16, stride=2), :] = jnp.where(left_half, a, pltpu.roll(c, 64, 1))
-            out_ref[pl.ds(y0 + 1, 16, stride=2), :] = jnp.where(
+            r = 2 * cy * lines
+            a, c = value[r : r + lines], value[r + lines : r + 2 * lines]
+            y0 = band * 128 + 64 * cy + row
+            out_ref[pl.ds(y0, lines, stride=2), :] = jnp.where(
+                left_half, a, pltpu.roll(c, 64, 1)
+            )
+            out_ref[pl.ds(y0 + 1, lines, stride=2), :] = jnp.where(
                 left_half, pltpu.roll(a, 64, 1), c
             )
 
     def fourth(n):
-        p, half = n % 3, n // 3
-        place(tbuf[n, pl.ds(pl.multiple_of(core * 64, 64), 64), :], 2 * p + core, half)
+        p, (half, first, width) = n % 3, PIECES[n // 3]
+        row, size = (half * HALF + first) // 64, width // 32
+        place(tbuf[n, pl.ds(pl.multiple_of(core * size, size), size), :], 2 * p + core, row)
         s4[n].wait_recv()
-        place(rbuf[n], 2 * p + 1 - core, half)
-        if half == 0:
+        place(rbuf[n, 0:size, :], 2 * p + 1 - core, row)
+        if n < UNITS - 3:
             return
         for b in (2 * p, 2 * p + 1):
             r = 128 * b
@@ -359,12 +394,12 @@
             halo.append(copy)
 
     steps = (reduce_tiles, second, third, fourth)
-    for n in range(6 + 6):
-        for lag, step in zip((0, 2, 4, 5), steps):
-            if 0 <= n - lag < 6:
+    for n in range(UNITS + LAGS[3] + 1):
+        for lag, step in zip(LAGS, steps):
+            if 0 <= n - lag < UNITS:
                 step(n - lag)
 
-    for n in range(NB):
+    for n in range(UNITS):
         for copy in s1[n][1] + s2[n] + s3[n] + [s4[n]]:
             copy.wait_send()
     for n, copy in enumerate(halo):
@@ -386,8 +421,8 @@
         out_specs=vmem,
         scratch_shapes=[
             pltpu.VMEM((NB, 128, 4096), BF16),
-            pltpu.VMEM((3, 128, 128), BF16),
-            pltpu.VMEM((3, 2, 64, 128), BF16),
+            pltpu.VMEM((3, 192, 128), BF16),
+            pltpu.VMEM((3, 64, 128), BF16),
             pltpu.VMEM((128, 128), F32),
             pltpu.VMEM((3, 2, 128, WIDE), BF16),
             pltpu.VMEM((3, 2, 128, HALF), BF16),
@@ -397,30 +432,30 @@
             pltpu.VMEM((3, 128, WIDE), BF16),
             pltpu.VMEM((NB, 128, HALF), F32),
             pltpu.VMEM((NB, 128, QUARTER), jnp.int32),
-            pltpu.VMEM((NB, 128, 128), F32),
+            pltpu.VMEM((UNITS, 128, 128), F32),
             pltpu.VMEM((NB, 3, 32, QUARTER), jnp.int32),
-            pltpu.VMEM((NB, 3, 32, 128), F32),
+            pltpu.VMEM((UNITS, 3, 32, 128), F32),
             pltpu.VMEM((NB, 32, HALF), F32),
             pltpu.VMEM((NB, 32, QUARTER), jnp.int32),
-            pltpu.VMEM((NB, 32, 128), F32),
+            pltpu.VMEM((UNITS, 32, 128), F32),
             pltpu.VMEM((NB, 3, 8, QUARTER), jnp.int32),
-            pltpu.VMEM((NB, 3, 8, 128), F32),
-            pltpu.VMEM((NB, 128, 128), F32),
-            pltpu.VMEM((NB, 64, 128), F32),
+            pltpu.VMEM((UNITS, 3, 8, 128), F32),
+            pltpu.VMEM((UNITS, 128, 128), F32),
+            pltpu.VMEM((UNITS, 64, 128), F32),
             pltpu.VMEM((4, NB, 8, 128), F32),
             pltpu.VMEM((8, NB, 8, 128), F32),
             dma((NB,)),
-            dma((NB, 2)),
-            dma((NB, 7)),
-            dma((NB, 7)),
+            dma((UNITS, 2)),
+            dma((UNITS, 7)),
+            dma((UNITS, 7)),
             dma((3, 7)),
             dma((3, 7)),
-            dma((NB, 3, 2)),
-            dma((NB, 3, 2)),
-            dma((NB, 3, 2)),
-            dma((NB, 3, 2)),
-            dma((NB,)),
-            dma((NB,)),
+            dma((UNITS, 3, 2)),
+            dma((UNITS, 3, 2)),
+            dma((UNITS, 3, 2)),
+            dma((UNITS, 3, 2)),
+            dma((UNITS,)),
+            dma((UNITS,)),
             dma((3, 8)),
             dma((3, 8)),
         ],
@@ -773,13 +808,17 @@
 
 def detect_kernel(
     taps_ref,
-    coadd_ref,
+    coadd_hbm,
     w1_ref,
     b1_ref,
     w2_ref,
     b2_ref,
-    psf_ref,
-    det_ref,
+    psf_hbm,
+    det_hbm,
+    coadd_ref,
+    psf_out,
+    det_out,
+    partial,
     ext,
     shifted,
     sides,
@@ -791,11 +830,15 @@
     turned,
     small,
     w2s,
+    sems,
 ):
     ix = lax.axis_index("skyx")
     iy = lax.axis_index("skyy")
     top, bottom = (iy > 0).astype(F32), (iy < 15).astype(F32)
     left, right = (ix > 0).astype(F32), (ix < 7).astype(F32)
+
+    fetch = pltpu.make_async_copy(coadd_hbm, coadd_ref, sems.at[0])
+    fetch.start()
 
     def halo(slot, b):
         r = 768 + slot * 48 + b * 8
@@ -817,6 +860,9 @@
     columns = small[...].T
     bias1 = jnp.broadcast_to(columns[0:64, 0:1], (64, 256))
     bias2 = jnp.broadcast_to(columns[0:64, 1:2], (64, 128))
+
+    taps3[...] = jnp.zeros_like(taps3)
+    fetch.wait()
 
     pieces = []
     for b in range(NB):
@@ -865,7 +911,6 @@
 
     sides[0:136, :] = edge_block(0, 136)
 
-    taps3[...] = jnp.zeros_like(taps3)
     for b in range(NB):
         ext[b, 8:136, :] = coadd_ref[128 * b : 128 * b + 128, :]
         ext[b, 0:8, :] = halo(1, b) * top
@@ -885,11 +930,21 @@
                 moved = pltpu.roll(jnp.where(column < j - 4, near_right, x), 132 - j, 1)
             shifted[j + 1] = moved
 
+        for n in range(6):
+            at_rows = slice(24 * n, 24 * n + 24)
+            sums = [None] * 9
+            for j in range(9):
+                value = shifted[j + 1, at_rows, :]
+                for i in range(9):
+                    term = taps_ref[i, b, j] * value
+                    sums[i] = term if j == 0 else sums[i] + term
+            for i in range(9):
+                partial[i, at_rows, :] = sums[i]
+
         def block(start, size):
-            acc = jnp.zeros((size, 128), F32)
-            for i in range(9):
-                for j in range(9):
-                    acc = acc + taps_ref[i, b, j] * shifted[j + 1, start + i : start + i + size, :]
+            acc = partial[0, start : start + size, :]
+            for i in range(1, 9):
+                acc = acc + partial[i, start + i : start + i + size, :]
             at = lax.broadcasted_iota(jnp.int32, (size, 128), 0) + start
             keep = jnp.where(at < 4, top, jnp.where(at >= 132, bottom, 1.0))
             v = acc.astype(BF16).astype(F32) * keep
@@ -908,10 +963,13 @@
 
         block(0, 72)
         block(72, 64)
-        psf_ref[b] = psf[4:132, :].astype(BF16)
+        psf_out[b] = psf[4:132, :].astype(BF16)
         return carry
 
     lax.fori_loop(0, NB, band, 0)
+
+    psf_copy = pltpu.make_async_copy(psf_out, psf_hbm, sems.at[1])
+    psf_copy.start()
 
     def silu(u):
         return u + u * jnp.tanh(u)
@@ -957,6 +1015,10 @@
     w2 = w2s[...]
     lane64 = lanes_of(64)
 
+    def leave(g):
+        at = pl.ds(pl.multiple_of(g * 16, 16), 16)
+        return pltpu.make_async_copy(det_out.at[g], det_hbm.at[:, at], sems.at[2 + g])
+
     def group(g, carry):
         def rows(n, inner):
             y = g * 16 + 2 * n
@@ -976,26 +1038,33 @@
                 )
             return inner
 
-        lax.fori_loop(0, 8, rows, 0, unroll=4)
-        det_ref[:, pl.ds(pl.multiple_of(g * 16, 16), 16), :] = (
-            turned[...].reshape(64, 16, 128).astype(BF16)
-        )
+        lax.fori_loop(0, 8, rows, 0, unroll=8)
+        det_out[g] = turned[...].reshape(64, 16, 128).astype(BF16)
+        leave(g).start()
         return carry
 
     lax.fori_loop(0, 8, group, 0)
+    psf_copy.wait()
+    for g in range(8):
+        leave(g).wait()
 
 
 def detect(taps, coadd, w1, b1, w2, b2):
     vmem = pl.BlockSpec(memory_space=pltpu.VMEM)
+    anywhere = pl.BlockSpec(memory_space=pl.ANY)
     return pl.pallas_call(
         detect_kernel,
         out_shape=(
             jax.ShapeDtypeStruct((NB, 128, 128), BF16),
             jax.ShapeDtypeStruct((64, 128, 128), BF16),
         ),
-        in_specs=[pl.BlockSpec(memory_space=pltpu.SMEM)] + [vmem] * 5,
-        out_specs=(vmem, vmem),
+        in_specs=[pl.BlockSpec(memory_space=pltpu.SMEM), anywhere] + [vmem] * 4,
+        out_specs=(anywhere, anywhere),
         scratch_shapes=[
+            pltpu.VMEM((1256, 128), F32),
+            pltpu.VMEM((NB, 128, 128), BF16),
+            pltpu.VMEM((8, 64, 16, 128), BF16),
+            pltpu.VMEM((9, 144, 128), F32),
             pltpu.VMEM((NB, 144, 128), F32),
             pltpu.VMEM((10, 144, 128), F32),
             pltpu.VMEM((144, 128), F32),
@@ -1007,6 +1076,7 @@
             pltpu.VMEM((64 * 16, 128), F32),
             pltpu.VMEM((128, 128), F32),
             pltpu.VMEM((192, 192), BF16),
+            pltpu.SemaphoreType.DMA((10,)),
         ],
         compiler_params=pltpu.CompilerParams(vmem_limit_bytes=48 * 1024 * 1024),
         name="detect",

time: 97.3 us -> 96 us (0.987)
  Pallas kernels: 95 us -> 93.5 us
    pallas_call x1, Pallas kernels: 18.7 us -> 17.6 us  [detect(): pl.pallas_call(detect_kernel, out_shape=(jax.ShapeDtypeStruct((NB, 128, 1...]
where the time goes in v5:
time: 96 us; the launch traced here: 95.8 us
  Pallas kernels  93.5 us (97%)
  between operations  1.59 us (2%)
    pallas_call x1, Pallas kernels, exchange(): pl.pallas_call(exchange_kernel, out_shape=jax.ShapeDtypeStruct((1256, 128...  75.9 us
    pallas_call x1, Pallas kernels, detect(): pl.pallas_call(detect_kernel, out_shape=(jax.ShapeDtypeStruct((NB, 128, 1...  17.6 us

profile of v5, /device:TPU:1, one launch (start us, length us, event | category | flops | bytes accessed | tf_op | source)
XLA Modules:
  0.0 95.8 jit_solution(11014055621532877256)
XLA Ops:
  0.6 0.0 copy-start.7
  0.6 0.0 copy-start.6
  0.7 0.0 copy-start.5
  0.7 0.0 copy-start
  0.7 0.0 copy-start.1
  0.7 0.0 copy-start.2
  0.7 0.0 copy-start.3
  0.7 0.0 copy-start.4
  0.7 75.9 %tile_exchange.1 = f32[1256,128]{1,0:T(8,128)S(1)} custom-call(bf16[6,128,4096]{2,1,0:T(8,128)(2,1)} %bitcast.15, bf16[6,128]{1,0:T(8,128)(2,1)} %bitcast.17, s32[1,128]{1,0:T(1,128)} %bitcast.19, s32[1,128]{1,0:T(1,128)} %bitcast.21), custom_call_target="tpu_custom_call" | custom-call | tf_op jit(solution)/shard_map/tile_exchange/pallas_call | solution.py:417
  76.6 0.5 slice.3
  77.8 0.0 copy-done.7
  77.8 0.0 copy-done.6
  77.8 0.0 copy-done.5
  77.8 0.2 conditional.1
  78.0 0.0 copy-done
  78.0 0.0 copy-done.1
  78.0 0.0 copy-done.2
  78.0 0.0 copy-done.3
  78.0 0.0 copy-done.4
  78.0 17.6 %detect.1 = (bf16[6,128,128]{2,1,0:T(8,128)(2,1)}, bf16[64,128,128]{2,1,0:T(8,128)(2,1)}) custom-call(f32[9,6,9]{2,1,0:T(8,128)S(1)} %bitcast.11, f32[1256,128]{1,0:T(8,128)S(1)} %get-tuple-element.18.coadd_hbm, bf16[6,3,3,64]{3,2,1,0:T(4,128)(2,1)S(1)} %bitcast.12, f32[1,64]{1,0:T(1,128)S(1)} %bitcast.13, bf16[3,3,64,64]{3,2,1,0:T(8,128)(2,1)S(1)} %bitcast.10, ...), custom_call_target="tpu_custom_call" | custom-call | tf_op jit(solution)/shard_map/detect/pallas_call | solution.py:1055
Async XLA Ops:
  0.6 77.1 %copy-start.7 = (s32[128]{0:T(128)S(1)}, s32[128]{0:T(128)}, u32[]{:S(2)}) copy-start(s32[128]{0:T(128)} %param.14) | copy-start | bytes 1540
  0.6 77.1 %copy-start.6 = (s32[128,1]{0,1:T(1,128)S(1)}, s32[128,1]{0,1:T(1,128)}, u32[]{:S(2)}) copy-start(s32[128,1]{0,1:T(1,128)} %param.13) | copy-start | bytes 1540
  0.7 77.1 %copy-start.5 = (bf16[128,6]{0,1:T(8,128)(2,1)S(1)}, bf16[128,6]{0,1:T(8,128)(2,1)}, u32[]{:S(2)}) copy-start(bf16[128,6]{0,1:T(8,128)(2,1)} %param.12) | copy-start | bytes 4612
  0.7 77.3 %copy-start = (bf16[64,64,3,3]{1,0,3,2:T(8,128)(2,1)S(1)}, bf16[64,64,3,3]{1,0,3,2:T(8,128)(2,1)}, u32[]{:S(2)}) copy-start(bf16[64,64,3,3]{1,0,3,2:T(8,128)(2,1)} %param.18) | copy-start | bytes 221188
  0.7 77.3 %copy-start.1 = (f32[6,9,9]{2,0,1:T(8,128)S(1)}, f32[6,9,9]{2,0,1:T(8,128)}, u32[]{:S(2)}) copy-start(f32[6,9,9]{2,0,1:T(8,128)} %param.15) | copy-start | bytes 5836
  0.7 77.3 %copy-start.2 = (bf16[64,6,3,3]{0,3,2,1:T(4,128)(2,1)S(1)}, bf16[64,6,3,3]{0,3,2,1:T(4,128)(2,1)}, u32[]{:S(2)}) copy-start(bf16[64,6,3,3]{0,3,2,1:T(4,128)(2,1)} %param.16) | copy-start | bytes 20740
  0.7 77.3 %copy-start.3 = (f32[64]{0:T(128)S(1)}, f32[64]{0:T(128)}, u32[]{:S(2)}) copy-start(f32[64]{0:T(128)} %param.17) | copy-start | bytes 772
  0.7 77.3 %copy-start.4 = (f32[64]{0:T(128)S(1)}, f32[64]{0:T(128)}, u32[]{:S(2)}) copy-start(f32[64]{0:T(128)} %param.19) | copy-start | bytes 772

commit v6 on v5

--- a/solution.py
+++ b/solution.py
@@ -829,6 +829,7 @@
     hidden,
     turned,
     small,
+    beside,
     w2s,
     sems,
 ):
@@ -852,14 +853,15 @@
         for i in range(3):
             small[pl.ds(i * 24 + b, 3, stride=8), 0:64] = w1_ref[b, i].astype(F32)
     w1 = (small[...].T[0:64, 0:72] * 0.5).astype(BF16)
-    for j in range(3):
-        for i in range(3):
-            w2s[64 * j : 64 * j + 64, 64 * i : 64 * i + 64] = w2_ref[i, j]
+    for i in range(3):
+        for j in range(3):
+            at = 64 * (3 * i + j)
+            w2s[:, at : at + 64] = w2_ref[i, j]
     small[0:1, 0:64] = b1_ref[...] * 0.5
     small[1:2, 0:64] = b2_ref[...]
     columns = small[...].T
     bias1 = jnp.broadcast_to(columns[0:64, 0:1], (64, 256))
-    bias2 = jnp.broadcast_to(columns[0:64, 1:2], (64, 128))
+    bias2 = jnp.broadcast_to(columns[0:64, 1:2], (64, 256))
 
     taps3[...] = jnp.zeros_like(taps3)
     fetch.wait()
@@ -974,26 +976,12 @@
     def silu(u):
         return u + u * jnp.tanh(u)
 
-    def first(n, carry):
-        at0 = pl.ds(pl.multiple_of((2 * n + 2) * 24, 8), 72)
-        at1 = pl.ds(pl.multiple_of((2 * n + 3) * 24, 8), 72)
-        rhs = jnp.concatenate([taps3[at0, :], taps3[at1, :]], axis=1).astype(BF16)
-        v = silu(jnp.dot(w1, rhs, preferred_element_type=F32) + bias1)
-        hidden[2 * n] = v[:, 0:128].astype(BF16)
-        hidden[2 * n + 1] = v[:, 128:256].astype(BF16)
-        return carry
-
-    lax.fori_loop(0, 65, first, 0, unroll=5)
-    hidden[0] = (hidden[0].astype(F32) * top).astype(BF16)
-    hidden[129] = (hidden[129].astype(F32) * bottom).astype(BF16)
-
     sides_t[0] = sides[0:128, :].T
     tail = jnp.concatenate([sides[128:136, :], jnp.zeros((120, 128), F32)], axis=0)
     sides_t[1] = tail.T
     edge3[...] = jnp.zeros_like(edge3)
     at256 = lax.broadcasted_iota(jnp.int32, (64, 256), 1)
     ends = jnp.where(at256 == 0, top, jnp.where(at256 == 129, bottom, 1.0))
-    beside = []
     for side, (offset, keep) in enumerate(((0, left), (9, right))):
         for t in range(2):
             for j in range(3):
@@ -1003,17 +991,37 @@
         x = edge3[side]
         rhs = jnp.concatenate([pltpu.roll(x, 256 - (2 + i), 1) for i in range(3)], axis=0)
         v = silu(jnp.dot(w1, rhs.astype(BF16), preferred_element_type=F32) + bias1)
-        v = (v * (ends * keep)).astype(BF16).astype(F32)
-        rhs = jnp.concatenate(
-            [v[:, 0:128]] + [pltpu.roll(v, 256 - i, 1)[:, 0:128] for i in (1, 2)], axis=0
-        )
-        weight = w2s[0:64, :] if side == 0 else w2s[128:192, :]
-        beside.append(jnp.dot(weight, rhs.astype(BF16), preferred_element_type=F32))
-    small[0:64, :] = beside[0]
-    small[64:128, :] = beside[1]
+        v = v * (ends * keep)
+        beside[side, 0] = v[:, 0:128]
+        beside[side, 1] = v[:, 128:256]
+
+    lane64 = lanes_of(64)
+
+    def pair(n, t):
+        at0 = pl.ds(pl.multiple_of((2 * n + 2) * 24, 8), 72)
+        at1 = pl.ds(pl.multiple_of((2 * n + 3) * 24, 8), 72)
+        rhs = jnp.concatenate([taps3[at0, :], taps3[at1, :]], axis=1).astype(BF16)
+        v = silu(jnp.dot(w1, rhs, preferred_element_type=F32) + bias1)
+        for k in range(2):
+            row, h = 2 * n + k, v[:, 128 * k : 128 * k + 128]
+            near = pltpu.roll(beside[0, t], 128 * (t + 1) - row, 1)
+            far = pltpu.roll(beside[1, t], 128 * (t + 1) - 1 - row, 1)
+            hidden[row, 0:64] = jnp.where(lane64 == 0, near, pltpu.roll(h, 1, 1)).astype(BF16)
+            hidden[row, 64:128] = h.astype(BF16)
+            hidden[row, 128:192] = jnp.where(lane64 == 127, far, pltpu.roll(h, 127, 1)).astype(
+                BF16
+            )
+
+    def first(n, carry):
+        pair(n, 0)
+        return carry
+
+    lax.fori_loop(0, 64, first, 0, unroll=16)
+    pair(64, 1)
+    hidden[0] = (hidden[0].astype(F32) * top).astype(BF16)
+    hidden[129] = (hidden[129].astype(F32) * bottom).astype(BF16)
 
     w2 = w2s[...]
-    lane64 = lanes_of(64)
 
     def leave(g):
         at = pl.ds(pl.multiple_of(g * 16, 16), 16)
@@ -1023,19 +1031,12 @@
         def rows(n, inner):
             y = g * 16 + 2 * n
             rhs = jnp.concatenate(
-                [hidden[pl.ds(y, 3)].reshape(192, 128), hidden[pl.ds(y + 1, 3)].reshape(192, 128)],
+                [hidden[pl.ds(y, 3)].reshape(576, 128), hidden[pl.ds(y + 1, 3)].reshape(576, 128)],
                 axis=1,
             )
-            z = jnp.dot(w2, rhs, preferred_element_type=F32)
-            for k in range(2):
-                c = slice(128 * k, 128 * k + 128)
-                near = pltpu.roll(small[0:64, :], 128 - (y + k), 1)
-                far = pltpu.roll(small[64:128, :], 127 - (y + k), 1)
-                before = jnp.where(lane64 == 0, near, pltpu.roll(z[0:64, c], 1, 1))
-                after = jnp.where(lane64 == 127, far, pltpu.roll(z[128:192, c], 127, 1))
-                turned[pl.ds(2 * n + k, 64, stride=16), :] = (before + z[64:128, c]) + (
-                    after + bias2
-                )
+            z = jnp.dot(w2, rhs, preferred_element_type=F32) + bias2
+            turned[pl.ds(2 * n, 64, stride=16), :] = z[:, 0:128]
+            turned[pl.ds(2 * n + 1, 64, stride=16), :] = z[:, 128:256]
             return inner
 
         lax.fori_loop(0, 8, rows, 0, unroll=8)
@@ -1072,10 +1073,11 @@
             pltpu.VMEM((136, 128), F32),
             pltpu.VMEM((136 * 24, 128), F32),
             pltpu.VMEM((2, 24, 256), F32),
-            pltpu.VMEM((130, 64, 128), BF16),
+            pltpu.VMEM((130, 192, 128), BF16),
             pltpu.VMEM((64 * 16, 128), F32),
             pltpu.VMEM((128, 128), F32),
-            pltpu.VMEM((192, 192), BF16),
+            pltpu.VMEM((2, 2, 64, 128), F32),
+            pltpu.VMEM((64, 576), BF16),
             pltpu.SemaphoreType.DMA((10,)),
         ],
         compiler_params=pltpu.CompilerParams(vmem_limit_bytes=48 * 1024 * 1024),

time: 96 us -> 95.2 us (level)
  no operation moved by 1% of the time
where the time goes in v6:
time: 95.2 us; the launch traced here: 95 us
  Pallas kernels  92.7 us (97%)
  between operations  1.59 us (2%)
    pallas_call x1, Pallas kernels, exchange(): pl.pallas_call(exchange_kernel, out_shape=jax.ShapeDtypeStruct((1256, 128...  75.9 us
    pallas_call x1, Pallas kernels, detect(): pl.pallas_call(detect_kernel, out_shape=(jax.ShapeDtypeStruct((NB, 128, 1...  16.8 us

profile of v6, /device:TPU:1, one launch (start us, length us, event | category | flops | bytes accessed | tf_op | source)
XLA Modules:
  0.0 95.0 jit_solution(2213319737106295236)
XLA Ops:
  0.6 0.0 copy-start.7
  0.6 0.0 copy-start.6
  0.7 0.0 copy-start.5
  0.7 0.0 copy-start
  0.7 0.0 copy-start.1
  0.7 0.0 copy-start.2
  0.7 0.0 copy-start.3
  0.7 0.0 copy-start.4
  0.7 75.9 %tile_exchange.1 = f32[1256,128]{1,0:T(8,128)S(1)} custom-call(bf16[6,128,4096]{2,1,0:T(8,128)(2,1)} %bitcast.15, bf16[6,128]{1,0:T(8,128)(2,1)} %bitcast.17, s32[1,128]{1,0:T(1,128)} %bitcast.19, s32[1,128]{1,0:T(1,128)} %bitcast.21), custom_call_target="tpu_custom_call" | custom-call | tf_op jit(solution)/shard_map/tile_exchange/pallas_call | solution.py:417
  76.6 0.5 slice.3
  77.8 0.0 copy-done.7
  77.8 0.0 copy-done.6
  77.8 0.0 copy-done.5
  77.8 0.2 conditional.1
  78.0 0.0 copy-done
  78.0 0.0 copy-done.1
  78.0 0.0 copy-done.2
  78.0 0.0 copy-done.3
  78.0 0.0 copy-done.4
  78.0 16.8 %detect.1 = (bf16[6,128,128]{2,1,0:T(8,128)(2,1)}, bf16[64,128,128]{2,1,0:T(8,128)(2,1)}) custom-call(f32[9,6,9]{2,1,0:T(8,128)S(1)} %bitcast.11, f32[1256,128]{1,0:T(8,128)S(1)} %get-tuple-element.18.coadd_hbm, bf16[6,3,3,64]{3,2,1,0:T(4,128)(2,1)S(1)} %bitcast.12, f32[1,64]{1,0:T(1,128)S(1)} %bitcast.13, bf16[3,3,64,64]{3,2,1,0:T(8,128)(2,1)S(1)} %bitcast.10, ...), custom_call_target="tpu_custom_call" | custom-call | tf_op jit(solution)/shard_map/detect/pallas_call | solution.py:1056
Async XLA Ops:
  0.6 77.1 %copy-start.7 = (s32[128]{0:T(128)S(1)}, s32[128]{0:T(128)}, u32[]{:S(2)}) copy-start(s32[128]{0:T(128)} %param.14) | copy-start | bytes 1540
  0.6 77.1 %copy-start.6 = (s32[128,1]{0,1:T(1,128)S(1)}, s32[128,1]{0,1:T(1,128)}, u32[]{:S(2)}) copy-start(s32[128,1]{0,1:T(1,128)} %param.13) | copy-start | bytes 1540
  0.7 77.1 %copy-start.5 = (bf16[128,6]{0,1:T(8,128)(2,1)S(1)}, bf16[128,6]{0,1:T(8,128)(2,1)}, u32[]{:S(2)}) copy-start(bf16[128,6]{0,1:T(8,128)(2,1)} %param.12) | copy-start | bytes 4612
  0.7 77.3 %copy-start = (bf16[64,64,3,3]{1,0,3,2:T(8,128)(2,1)S(1)}, bf16[64,64,3,3]{1,0,3,2:T(8,128)(2,1)}, u32[]{:S(2)}) copy-start(bf16[64,64,3,3]{1,0,3,2:T(8,128)(2,1)} %param.18) | copy-start | bytes 221188
  0.7 77.3 %copy-start.1 = (f32[6,9,9]{2,0,1:T(8,128)S(1)}, f32[6,9,9]{2,0,1:T(8,128)}, u32[]{:S(2)}) copy-start(f32[6,9,9]{2,0,1:T(8,128)} %param.15) | copy-start | bytes 5836
  0.7 77.3 %copy-start.2 = (bf16[64,6,3,3]{0,3,2,1:T(4,128)(2,1)S(1)}, bf16[64,6,3,3]{0,3,2,1:T(4,128)(2,1)}, u32[]{:S(2)}) copy-start(bf16[64,6,3,3]{0,3,2,1:T(4,128)(2,1)} %param.16) | copy-start | bytes 20740
  0.7 77.3 %copy-start.3 = (f32[64]{0:T(128)S(1)}, f32[64]{0:T(128)}, u32[]{:S(2)}) copy-start(f32[64]{0:T(128)} %param.17) | copy-start | bytes 772
  0.7 77.3 %copy-start.4 = (f32[64]{0:T(128)S(1)}, f32[64]{0:T(128)}, u32[]{:S(2)}) copy-start(f32[64]{0:T(128)} %param.19) | copy-start | bytes 772

commit v7 on v6

--- a/solution.py
+++ b/solution.py
@@ -17,7 +17,7 @@
 WIDE = HALF + 128
 PIECES = ((0, 0, 2048), (1, 0, 2048))
 UNITS = 3 * len(PIECES)
-LAGS = (0, 2, 4, 5)
+LAGS = (0, 3, 5, 6)
 ORDER = (0, 2, 4, 1, 3, 5)
 MEMBERS = ((2, 0), (2, 1), (1, 0), (3, 0), (1, 1), (3, 1), (0, 1))
 AROUND = ((-1, 0), (1, 0), (0, -1), (0, 1), (-1, -1), (-1, 1), (1, -1), (1, 1))
@@ -1016,7 +1016,7 @@
         pair(n, 0)
         return carry
 
-    lax.fori_loop(0, 64, first, 0, unroll=16)
+    lax.fori_loop(0, 64, first, 0, unroll=32)
     pair(64, 1)
     hidden[0] = (hidden[0].astype(F32) * top).astype(BF16)
     hidden[129] = (hidden[129].astype(F32) * bottom).astype(BF16)

time: 95.2 us -> 94.8 us (level)
  no operation moved by 1% of the time
where the time goes in v7:
time: 94.8 us; the launch traced here: 94.6 us
  Pallas kernels  92.3 us (97%)
  between operations  1.59 us (2%)
    pallas_call x1, Pallas kernels, exchange(): pl.pallas_call(exchange_kernel, out_shape=jax.ShapeDtypeStruct((1256, 128...  75.7 us
    pallas_call x1, Pallas kernels, detect(): pl.pallas_call(detect_kernel, out_shape=(jax.ShapeDtypeStruct((NB, 128, 1...  16.6 us

profile of v7, /device:TPU:1, one launch (start us, length us, event | category | flops | bytes accessed | tf_op | source)
XLA Modules:
  0.0 94.6 jit_solution(5479237548369292220)
XLA Ops:
  0.6 0.0 copy-start.7
  0.6 0.0 copy-start.6
  0.7 0.0 copy-start.5
  0.7 0.0 copy-start
  0.7 0.0 copy-start.1
  0.7 0.0 copy-start.2
  0.7 0.0 copy-start.3
  0.7 0.0 copy-start.4
  0.7 75.7 %tile_exchange.1 = f32[1256,128]{1,0:T(8,128)S(1)} custom-call(bf16[6,128,4096]{2,1,0:T(8,128)(2,1)} %bitcast.15, bf16[6,128]{1,0:T(8,128)(2,1)} %bitcast.17, s32[1,128]{1,0:T(1,128)} %bitcast.19, s32[1,128]{1,0:T(1,128)} %bitcast.21), custom_call_target="tpu_custom_call" | custom-call | tf_op jit(solution)/shard_map/tile_exchange/pallas_call | solution.py:417
  76.5 0.5 slice.3
  77.6 0.0 copy-done.7
  77.6 0.0 copy-done.6
  77.6 0.0 copy-done.5
  77.7 0.2 conditional.1
  77.8 0.0 copy-done
  77.9 0.0 copy-done.1
  77.9 0.0 copy-done.2
  77.9 0.0 copy-done.3
  77.9 0.0 copy-done.4
  77.9 16.6 %detect.1 = (bf16[6,128,128]{2,1,0:T(8,128)(2,1)}, bf16[64,128,128]{2,1,0:T(8,128)(2,1)}) custom-call(f32[9,6,9]{2,1,0:T(8,128)S(1)} %bitcast.11, f32[1256,128]{1,0:T(8,128)S(1)} %get-tuple-element.18.coadd_hbm, bf16[6,3,3,64]{3,2,1,0:T(4,128)(2,1)S(1)} %bitcast.12, f32[1,64]{1,0:T(1,128)S(1)} %bitcast.13, bf16[3,3,64,64]{3,2,1,0:T(8,128)(2,1)S(1)} %bitcast.10, ...), custom_call_target="tpu_custom_call" | custom-call | tf_op jit(solution)/shard_map/detect/pallas_call | solution.py:1056
Async XLA Ops:
  0.6 77.0 %copy-start.7 = (s32[128]{0:T(128)S(1)}, s32[128]{0:T(128)}, u32[]{:S(2)}) copy-start(s32[128]{0:T(128)} %param.14) | copy-start | bytes 1540
  0.6 77.0 %copy-start.6 = (s32[128,1]{0,1:T(1,128)S(1)}, s32[128,1]{0,1:T(1,128)}, u32[]{:S(2)}) copy-start(s32[128,1]{0,1:T(1,128)} %param.13) | copy-start | bytes 1540
  0.7 77.0 %copy-start.5 = (bf16[128,6]{0,1:T(8,128)(2,1)S(1)}, bf16[128,6]{0,1:T(8,128)(2,1)}, u32[]{:S(2)}) copy-start(bf16[128,6]{0,1:T(8,128)(2,1)} %param.12) | copy-start | bytes 4612
  0.7 77.2 %copy-start = (bf16[64,64,3,3]{1,0,3,2:T(8,128)(2,1)S(1)}, bf16[64,64,3,3]{1,0,3,2:T(8,128)(2,1)}, u32[]{:S(2)}) copy-start(bf16[64,64,3,3]{1,0,3,2:T(8,128)(2,1)} %param.18) | copy-start | bytes 221188
  0.7 77.2 %copy-start.1 = (f32[6,9,9]{2,0,1:T(8,128)S(1)}, f32[6,9,9]{2,0,1:T(8,128)}, u32[]{:S(2)}) copy-start(f32[6,9,9]{2,0,1:T(8,128)} %param.15) | copy-start | bytes 5836
  0.7 77.2 %copy-start.2 = (bf16[64,6,3,3]{0,3,2,1:T(4,128)(2,1)S(1)}, bf16[64,6,3,3]{0,3,2,1:T(4,128)(2,1)}, u32[]{:S(2)}) copy-start(bf16[64,6,3,3]{0,3,2,1:T(4,128)(2,1)} %param.16) | copy-start | bytes 20740
  0.7 77.2 %copy-start.3 = (f32[64]{0:T(128)S(1)}, f32[64]{0:T(128)}, u32[]{:S(2)}) copy-start(f32[64]{0:T(128)} %param.17) | copy-start | bytes 772
  0.7 77.2 %copy-start.4 = (f32[64]{0:T(128)S(1)}, f32[64]{0:T(128)}, u32[]{:S(2)}) copy-start(f32[64]{0:T(128)} %param.19) | copy-start | bytes 772

commit v8 on v7

--- a/solution.py
+++ b/solution.py
@@ -290,7 +290,7 @@
             acc2[m, :, at] = pick(c, src[p, :, at]) + pick(cx, recv_x[p, :, at])
             return carry
 
-        lax.fori_loop(0, width // 512, reduce, 0)
+        lax.fori_loop(0, width // 512, reduce, 0, unroll=2)
         words, extra = encode(acc2[m, :, first : first + width], denom, flag, 128)
         st2[m, :, first // 2 : (first + width) // 2] = words
         st2m[n] = extra

time: 94.8 us -> 94.2 us (level)
  no operation moved by 1% of the time
where the time goes in v8:
time: 94.2 us; the launch traced here: 94.1 us
  Pallas kernels  91.8 us (97%)
  between operations  1.59 us (2%)
    pallas_call x1, Pallas kernels, exchange(): pl.pallas_call(exchange_kernel, out_shape=jax.ShapeDtypeStruct((1256, 128...  75.2 us
    pallas_call x1, Pallas kernels, detect(): pl.pallas_call(detect_kernel, out_shape=(jax.ShapeDtypeStruct((NB, 128, 1...  16.6 us

profile of v8, /device:TPU:1, one launch (start us, length us, event | category | flops | bytes accessed | tf_op | source)
XLA Modules:
  0.0 94.1 jit_solution(16191914569784894494)
XLA Ops:
  0.6 0.0 copy-start.7
  0.6 0.0 copy-start.6
  0.7 0.0 copy-start.5
  0.7 0.0 copy-start
  0.7 0.0 copy-start.1
  0.7 0.0 copy-start.2
  0.7 0.0 copy-start.3
  0.7 0.0 copy-start.4
  0.7 75.2 %tile_exchange.1 = f32[1256,128]{1,0:T(8,128)S(1)} custom-call(bf16[6,128,4096]{2,1,0:T(8,128)(2,1)} %bitcast.15, bf16[6,128]{1,0:T(8,128)(2,1)} %bitcast.17, s32[1,128]{1,0:T(1,128)} %bitcast.19, s32[1,128]{1,0:T(1,128)} %bitcast.21), custom_call_target="tpu_custom_call" | custom-call | tf_op jit(solution)/shard_map/tile_exchange/pallas_call | solution.py:417
  75.9 0.5 slice.3
  77.1 0.0 copy-done.7
  77.1 0.0 copy-done.6
  77.1 0.0 copy-done.5
  77.1 0.2 conditional.1
  77.3 0.0 copy-done
  77.3 0.0 copy-done.1
  77.3 0.0 copy-done.2
  77.3 0.0 copy-done.3
  77.3 0.0 copy-done.4
  77.3 16.6 %detect.1 = (bf16[6,128,128]{2,1,0:T(8,128)(2,1)}, bf16[64,128,128]{2,1,0:T(8,128)(2,1)}) custom-call(f32[9,6,9]{2,1,0:T(8,128)S(1)} %bitcast.11, f32[1256,128]{1,0:T(8,128)S(1)} %get-tuple-element.18.coadd_hbm, bf16[6,3,3,64]{3,2,1,0:T(4,128)(2,1)S(1)} %bitcast.12, f32[1,64]{1,0:T(1,128)S(1)} %bitcast.13, bf16[3,3,64,64]{3,2,1,0:T(8,128)(2,1)S(1)} %bitcast.10, ...), custom_call_target="tpu_custom_call" | custom-call | tf_op jit(solution)/shard_map/detect/pallas_call | solution.py:1056
Async XLA Ops:
  0.6 76.4 %copy-start.7 = (s32[128]{0:T(128)S(1)}, s32[128]{0:T(128)}, u32[]{:S(2)}) copy-start(s32[128]{0:T(128)} %param.14) | copy-start | bytes 1540
  0.6 76.4 %copy-start.6 = (s32[128,1]{0,1:T(1,128)S(1)}, s32[128,1]{0,1:T(1,128)}, u32[]{:S(2)}) copy-start(s32[128,1]{0,1:T(1,128)} %param.13) | copy-start | bytes 1540
  0.7 76.4 %copy-start.5 = (bf16[128,6]{0,1:T(8,128)(2,1)S(1)}, bf16[128,6]{0,1:T(8,128)(2,1)}, u32[]{:S(2)}) copy-start(bf16[128,6]{0,1:T(8,128)(2,1)} %param.12) | copy-start | bytes 4612
  0.7 76.6 %copy-start = (bf16[64,64,3,3]{1,0,3,2:T(8,128)(2,1)S(1)}, bf16[64,64,3,3]{1,0,3,2:T(8,128)(2,1)}, u32[]{:S(2)}) copy-start(bf16[64,64,3,3]{1,0,3,2:T(8,128)(2,1)} %param.18) | copy-start | bytes 221188
  0.7 76.6 %copy-start.1 = (f32[6,9,9]{2,0,1:T(8,128)S(1)}, f32[6,9,9]{2,0,1:T(8,128)}, u32[]{:S(2)}) copy-start(f32[6,9,9]{2,0,1:T(8,128)} %param.15) | copy-start | bytes 5836
  0.7 76.6 %copy-start.2 = (bf16[64,6,3,3]{0,3,2,1:T(4,128)(2,1)S(1)}, bf16[64,6,3,3]{0,3,2,1:T(4,128)(2,1)}, u32[]{:S(2)}) copy-start(bf16[64,6,3,3]{0,3,2,1:T(4,128)(2,1)} %param.16) | copy-start | bytes 20740
  0.7 76.6 %copy-start.3 = (f32[64]{0:T(128)S(1)}, f32[64]{0:T(128)}, u32[]{:S(2)}) copy-start(f32[64]{0:T(128)} %param.17) | copy-start | bytes 772
  0.7 76.6 %copy-start.4 = (f32[64]{0:T(128)S(1)}, f32[64]{0:T(128)}, u32[]{:S(2)}) copy-start(f32[64]{0:T(128)} %param.19) | copy-start | bytes 772
